TPU v7x, 512 devices: a whole 4x4x16 slice. The times are simulated.
512 devices in a mesh: path: 2 (over core), lon: 32 (over z_hi, x, y), lat: 8 (over z_lo).
Axes of the slice: x: 4, y: 4, z: 16 (z_hi: 2, z_lo: 8; z = z_hi * 8 + z_lo), core: 2. Of those that a mesh axis runs over, the one named last changes fastest.
Arguments:
- observed: bfloat16 [512, 128, 384], P('lon', 'lat'), may hold values from -6 to 6
- baseline: bfloat16 [512, 128, 384], P('lon', 'lat'), may hold values from -6 to 6
- cotangent: bfloat16 [512, 128, 384], P('lon', 'lat'), may hold values from -6 to 6
- first_weight: bfloat16 [9, 384, 384], P(None, 'path'), may hold values from -0.109375 to 0.109375
- first_bias: float32 [384], replicated, may hold values from -3 to 3
- second_weight: bfloat16 [9, 384, 384], P(None, 'path'), may hold values from -0.109375 to 0.109375
- second_bias: float32 [384], replicated, may hold values from -3 to 3
Outputs:
- attribution: bfloat16 [512, 128, 384], P(('lon', 'path'), 'lat')
All inputs are finite; a program needn't handle non-finite values.
Results may differ from a plain program's by a relative error of at most 0.0038.
Values may be sent and summed in bfloat16 or wider, within the bound.
A program may use at most 64 MiB of HBM per device.

v0:
```python
import jax
import jax.numpy as jnp
from jax import lax
from jax.sharding import PartitionSpec as P

NEAR = 4
FAR = 16


def padded_2(cells, sides, width):
    for axis, dim in sides:
        count = lax.axis_size(axis)
        ends = count - 1
        head = lax.slice_in_dim(cells, 0, width, axis=dim)
        tail = lax.slice_in_dim(cells, cells.shape[dim] - width, cells.shape[dim], axis=dim)
        cells = jnp.concatenate(
            [
                lax.ppermute(tail, axis, [(i, (i + 1) % count) for i in range(ends)]),
                cells,
                lax.ppermute(head, axis, [((i + 1) % count, i) for i in range(ends)]),
            ],
            axis=dim,
        )
    return cells


def smooth_act(value):
    return jax.nn.gelu(value, approximate=True)


def act_adjoint(pre_value, upstream):
    unused, pullback = jax.vjp(smooth_act, pre_value)
    return pullback(upstream)[0]


def stencil(padded, weights, dilation, rows, cols, forward):
    accumulated = jnp.zeros((rows, cols, weights.shape[1]), jnp.float32)
    for offset_row in (-1, 0, 1):
        for offset_col in (-1, 0, 1):
            tap_index = (offset_row + 1) * 3 + offset_col + 1
            sign = 1 if forward else -1
            start_row = dilation + sign * offset_row * dilation
            start_col = dilation + sign * offset_col * dilation
            window = padded[start_row : start_row + rows, start_col : start_col + cols, :]
            if forward:
                accumulated = accumulated + jnp.dot(
                    window, weights[tap_index], preferred_element_type=jnp.float32
                )
            else:
                accumulated = accumulated + lax.dot_general(
                    window,
                    weights[tap_index],
                    (((2,), (1,)), ((), ())),
                    preferred_element_type=jnp.float32,
                )
    return accumulated


def shards(observed, baseline, cotangent, first_weight, first_bias, second_weight, second_bias):
    rows, cols = (observed.shape[0], observed.shape[1])
    first_full, second_full = (
        lax.all_gather(first_weight, "path", axis=1, tiled=True),
        lax.all_gather(second_weight, "path", axis=1, tiled=True),
    )
    diff = observed.astype(jnp.float32) - baseline.astype(jnp.float32)
    upstream = cotangent.astype(jnp.float32)
    points = lax.axis_size("path")
    mix_weight = (lax.axis_index("path").astype(jnp.float32) + 0.5) / points
    point_field = (baseline.astype(jnp.float32) + mix_weight * diff).astype(jnp.bfloat16)
    point_padded = padded_2(point_field, (("lon", 0), ("lat", 1)), NEAR)
    first_pre = stencil(point_padded, first_full, NEAR, rows, cols, True) + first_bias
    hidden = (point_field.astype(jnp.float32) + smooth_act(first_pre)).astype(jnp.bfloat16)
    hidden_padded = padded_2(hidden, (("lon", 0), ("lat", 1)), FAR)
    second_pre = stencil(hidden_padded, second_full, FAR, rows, cols, True) + second_bias
    second_adj = act_adjoint(second_pre, upstream).astype(jnp.bfloat16)
    second_padded = padded_2(second_adj, (("lon", 0), ("lat", 1)), FAR)
    hidden_adj = upstream + stencil(second_padded, second_full, FAR, rows, cols, False)
    first_adj = act_adjoint(first_pre, hidden_adj).astype(jnp.bfloat16)
    first_padded = padded_2(first_adj, (("lon", 0), ("lat", 1)), NEAR)
    point_grad = hidden_adj + stencil(first_padded, first_full, NEAR, rows, cols, False)
    half_rows = rows // points
    row_start = lax.axis_index("path") * half_rows
    diff_rows = lax.dynamic_slice_in_dim(diff, row_start, half_rows, 0)
    grad_whole = lax.psum(point_grad, "path")
    grad_rows = lax.dynamic_slice_in_dim(grad_whole, row_start, half_rows, 0)
    return (diff_rows * grad_rows / points).astype(jnp.bfloat16)


def solution(mesh):
    placed = (
        P("lon", "lat", None),
        P("lon", "lat", None),
        P("lon", "lat", None),
        P(None, "path", None),
        P(),
        P(None, "path", None),
        P(),
    )
    return jax.shard_map(
        shards,
        mesh=mesh,
        in_specs=placed,
        out_specs=P(("lon", "path"), "lat", None),
        check_vma=False,
    )
```

profile of v0, /device:TPU:1, one launch (start us, length us, event | category | flops | bytes accessed | tf_op | source)
XLA Modules:
  0.0 251.0 jit_solution(17287451170244009545)
XLA Ops:
  7.3 1.8 convert_subtract_fusion
  9.2 4.0 %collective-permute-start = (bf16[4,16,384]{2,1,0:T(8,128)(2,1)S(1)}, bf16[4,16,384]{2,1,0:T(8,128)(2,1)S(1)}, u32[]{:S(2)}, u32[]{:S(2)}) collective-permute-start(bf16[4,16,384]{2,1,0:T(8,128)(2,1)S(1)} %get-tuple-element.17), channel_id=1, source_target_pairs={{0,8},{8,16},{16,24},{24,32},{32,40},{40,48},{48,56},{56,64},{64,7... | collective-permute-start | bytes 147464 | tf_op jit(solution)/shard_map/ppermute | solution.py:18
  13.2 1.3 collective-permute-start.1
  14.5 3.5 %collective-permute-done.1 = bf16[4,16,384]{2,1,0:T(8,128)(2,1)S(1)} collective-permute-done((bf16[4,16,384]{2,1,0:T(8,128)(2,1)S(1)}, bf16[4,16,384]{2,1,0:T(8,128)(2,1)S(1)}, u32[]{:S(2)}, u32[]{:S(2)}) %collective-permute-start.1) | collective-permute-done | bytes 49184 | tf_op jit(solution)/shard_map/ppermute | solution.py:20
  18.1 3.5 %collective-permute-start.2 = (bf16[24,4,384]{2,1,0:T(4,128)(2,1)S(1)}, bf16[24,4,384]{2,1,0:T(4,128)(2,1)S(1)}, u32[]{:S(2)}, u32[]{:S(2)}) collective-permute-start(bf16[24,4,384]{2,1,0:T(4,128)(2,1)S(1)} %get-tuple-element.13), channel_id=1, source_target_pairs={{0,1},{1,2},{2,3},{3,4},{4,5},{5,6},{6,7},{8,9},{9,10},{10,11},{11... | collective-permute-start | bytes 221192 | tf_op jit(solution)/shard_map/ppermute | solution.py:18
  21.6 1.3 collective-permute-start.3
  23.0 3.9 %collective-permute-done.3 = bf16[24,4,384]{2,1,0:T(4,128)(2,1)S(1)} collective-permute-done((bf16[24,4,384]{2,1,0:T(4,128)(2,1)S(1)}, bf16[24,4,384]{2,1,0:T(4,128)(2,1)S(1)}, u32[]{:S(2)}, u32[]{:S(2)}) %collective-permute-start.3) | collective-permute-done | bytes 73760 | tf_op jit(solution)/shard_map/ppermute | solution.py:20
  27.9 10.1 %all-gather.3.cloned.1.call-done = bf16[9,384,384]{2,1,0:T(8,128)(2,1)} async-done(((bf16[9,192,384]{2,1,0:T(8,128)(2,1)}), bf16[9,384,384]{2,1,0:T(8,128)(2,1)}) %all-gather.3.cloned.1.call-update) | async-done | bytes 2654224 | tf_op jit(solution)/shard_map/all_gather | solution.py:62
  38.1 1.4 fusion.47
  43.8 2.1 collective-permute-start.4
  45.9 1.3 collective-permute-start.5
  47.2 2.7 %collective-permute-done.4 = bf16[16,16,384]{2,1,0:T(8,128)(2,1)S(1)} collective-permute-done((bf16[16,16,384]{2,1,0:T(8,128)(2,1)S(1)}, bf16[16,16,384]{2,1,0:T(8,128)(2,1)S(1)}, u32[]{:S(2)}, u32[]{:S(2)}) %collective-permute-start.4) | collective-permute-done | bytes 196640 | tf_op jit(solution)/shard_map/ppermute | solution.py:18
  49.9 4.0 %collective-permute-done.5 = bf16[16,16,384]{2,1,0:T(8,128)(2,1)} collective-permute-done((bf16[16,16,384]{2,1,0:T(8,128)(2,1)S(1)}, bf16[16,16,384]{2,1,0:T(8,128)(2,1)}, u32[]{:S(2)}, u32[]{:S(2)}) %collective-permute-start.5) | collective-permute-done | bytes 196640 | tf_op jit(solution)/shard_map/ppermute | solution.py:20
  53.9 1.8 pad_maximum_fusion
  55.7 4.0 %collective-permute-start.6 = (bf16[48,16,384]{2,1,0:T(8,128)(2,1)}, bf16[48,16,384]{2,1,0:T(8,128)(2,1)}, u32[]{:S(2)}, u32[]{:S(2)}) collective-permute-start(bf16[48,16,384]{2,1,0:T(8,128)(2,1)} %pad_maximum_fusion), channel_id=1, source_target_pairs={{0,1},{1,2},{2,3},{3,4},{4,5},{5,6},{6,7},{8,9},{9,10},{10,11},{11... | collective-permute-start | bytes 1769480 | tf_op jit(solution)/shard_map/ppermute | solution.py:18
  59.7 7.8 %all-gather.5.cloned.1.call-done = bf16[9,384,384]{2,1,0:T(8,128)(2,1)} async-done(((bf16[9,192,384]{2,1,0:T(8,128)(2,1)}), bf16[9,384,384]{2,1,0:T(8,128)(2,1)}) %all-gather.5.cloned.1.call-update) | async-done | bytes 2654224 | tf_op jit(solution)/shard_map/all_gather | solution.py:63
  67.6 1.4 fusion.67
  69.0 1.3 collective-permute-start.7
  71.5 1.3 fusion.71
  72.8 1.3 fusion.65
  75.4 10.3 %collective-permute-done.7 = bf16[48,16,384]{2,1,0:T(8,128)(2,1)S(1)} collective-permute-done((bf16[48,16,384]{2,1,0:T(8,128)(2,1)}, bf16[48,16,384]{2,1,0:T(8,128)(2,1)S(1)}, u32[]{:S(2)}, u32[]{:S(2)}) %collective-permute-start.7) | collective-permute-done | bytes 589856 | tf_op jit(solution)/shard_map/ppermute | solution.py:20
  88.1 2.1 collective-permute-start.8
  90.2 1.3 collective-permute-start.9
  91.5 1.9 collective-permute-done.8
  93.4 3.8 %collective-permute-done.9 = bf16[16,16,384]{2,1,0:T(8,128)(2,1)S(1)} collective-permute-done((bf16[16,16,384]{2,1,0:T(8,128)(2,1)S(1)}, bf16[16,16,384]{2,1,0:T(8,128)(2,1)S(1)}, u32[]{:S(2)}, u32[]{:S(2)}) %collective-permute-start.9) | collective-permute-done | bytes 196640 | tf_op jit(solution)/shard_map/ppermute | solution.py:20
  98.9 4.0 %collective-permute-start.11 = (bf16[48,16,384]{2,1,0:T(8,128)(2,1)S(1)}, bf16[48,16,384]{2,1,0:T(8,128)(2,1)S(1)}, u32[]{:S(2)}, u32[]{:S(2)}) collective-permute-start(bf16[48,16,384]{2,1,0:T(8,128)(2,1)S(1)} %pad_maximum_fusion.1), channel_id=1, source_target_pairs={{0,1},{1,2},{2,3},{3,4},{4,5},{5,6},{6,7},{8,9},{9,10},{10,11},{11... | collective-permute-start | bytes 1769480 | tf_op jit(solution)/shard_map/ppermute | solution.py:18
  103.5 8.4 %collective-permute-done.10 = bf16[48,16,384]{2,1,0:T(8,128)(2,1)S(1)} collective-permute-done((bf16[48,16,384]{2,1,0:T(8,128)(2,1)S(1)}, bf16[48,16,384]{2,1,0:T(8,128)(2,1)S(1)}, u32[]{:S(2)}, u32[]{:S(2)}) %collective-permute-start.10) | collective-permute-done | bytes 589856 | tf_op jit(solution)/shard_map/ppermute | solution.py:20
  115.8 4.0 %collective-permute-start.12 = (bf16[4,16,384]{2,1,0:T(8,128)(2,1)S(1)}, bf16[4,16,384]{2,1,0:T(8,128)(2,1)S(1)}, u32[]{:S(2)}, u32[]{:S(2)}) collective-permute-start(bf16[4,16,384]{2,1,0:T(8,128)(2,1)S(1)} %get-tuple-element.15), channel_id=1, source_target_pairs={{0,8},{8,16},{16,24},{24,32},{32,40},{40,48},{48,56},{56,64},{64,7... | collective-permute-start | bytes 147464 | tf_op jit(solution)/shard_map/ppermute | solution.py:18
  121.0 1.3 collective-permute-start.14
  122.3 4.7 %collective-permute-start.15 = (bf16[24,4,384]{2,1,0:T(4,128)(2,1)S(1)}, bf16[24,4,384]{2,1,0:T(4,128)(2,1)S(1)}, u32[]{:S(2)}, u32[]{:S(2)}) collective-permute-start(bf16[24,4,384]{2,1,0:T(4,128)(2,1)S(1)} %get-tuple-element.10), channel_id=1, source_target_pairs={{0,1},{1,2},{2,3},{3,4},{4,5},{5,6},{6,7},{8,9},{9,10},{10,11},{11... | collective-permute-start | bytes 221192 | tf_op jit(solution)/shard_map/ppermute | solution.py:18
  131.3 111.6 %all-reduce.2.cloned.1.call-done = f32[16,16,384]{2,1,0:T(8,128)} async-done(((f32[16,16,384]{2,1,0:T(8,128)}), f32[16,16,384]{2,1,0:T(8,128)}) %all-reduce.2.cloned.1.call-update) | async-done | bytes 393232 | tf_op jit(solution)/shard_map/psum | solution.py:84
  242.9 1.6 multiply_convert_fusion
  (69 shorter events, 22.4 us)
Async XLA Ops:
  6.5 31.5 %all-gather.3.cloned.1.call-start = ((), (), s32[]{:S(2)}) async-start(), calls=%async_computation | async-start | bytes 3981312 | tf_op jit(solution)/shard_map/all_gather | solution.py:62
  7.3 60.3 %all-gather.5.cloned.1.call-start = ((), (), s32[]{:S(2)}) async-start(), calls=%async_computation.1 | async-start | bytes 3981312 | tf_op jit(solution)/shard_map/all_gather | solution.py:63
  9.2 5.3 %collective-permute-start = (bf16[4,16,384]{2,1,0:T(8,128)(2,1)S(1)}, bf16[4,16,384]{2,1,0:T(8,128)(2,1)S(1)}, u32[]{:S(2)}, u32[]{:S(2)}) collective-permute-start(bf16[4,16,384]{2,1,0:T(8,128)(2,1)S(1)} %get-tuple-element.17), channel_id=1, source_target_pairs={{0,8},{8,16},{16,24},{24,32},{32,40},{40,48},{48,56},{56,64},{64,7... | collective-permute-start | bytes 147464 | tf_op jit(solution)/shard_map/ppermute | solution.py:18
  13.2 4.8 %collective-permute-start.1 = (bf16[4,16,384]{2,1,0:T(8,128)(2,1)S(1)}, bf16[4,16,384]{2,1,0:T(8,128)(2,1)S(1)}, u32[]{:S(2)}, u32[]{:S(2)}) collective-permute-start(bf16[4,16,384]{2,1,0:T(8,128)(2,1)S(1)} %get-tuple-element.18), channel_id=1, source_target_pairs={{8,0},{16,8},{24,16},{32,24},{40,32},{48,40},{56,48},{64,56},{72,6... | collective-permute-start | bytes 147464 | tf_op jit(solution)/shard_map/ppermute | solution.py:20
  18.1 4.9 %collective-permute-start.2 = (bf16[24,4,384]{2,1,0:T(4,128)(2,1)S(1)}, bf16[24,4,384]{2,1,0:T(4,128)(2,1)S(1)}, u32[]{:S(2)}, u32[]{:S(2)}) collective-permute-start(bf16[24,4,384]{2,1,0:T(4,128)(2,1)S(1)} %get-tuple-element.13), channel_id=1, source_target_pairs={{0,1},{1,2},{2,3},{3,4},{4,5},{5,6},{6,7},{8,9},{9,10},{10,11},{11... | collective-permute-start | bytes 221192 | tf_op jit(solution)/shard_map/ppermute | solution.py:18
  21.6 5.3 %collective-permute-start.3 = (bf16[24,4,384]{2,1,0:T(4,128)(2,1)S(1)}, bf16[24,4,384]{2,1,0:T(4,128)(2,1)S(1)}, u32[]{:S(2)}, u32[]{:S(2)}) collective-permute-start(bf16[24,4,384]{2,1,0:T(4,128)(2,1)S(1)} %get-tuple-element.14), channel_id=1, source_target_pairs={{1,0},{2,1},{3,2},{4,3},{5,4},{6,5},{7,6},{9,8},{10,9},{11,10},{12... | collective-permute-start | bytes 221192 | tf_op jit(solution)/shard_map/ppermute | solution.py:20
  23.0 219.9 %all-reduce.2.cloned.1.call-start = ((), (), s32[]{:S(2)}) async-start(), calls=%async_computation.2 | async-start | bytes 786432 | tf_op jit(solution)/shard_map/psum | solution.py:84
  38.1 3.9 %copy-start.1 = (bf16[9,384,384]{2,1,0:T(8,128)(2,1)S(1)}, bf16[9,384,384]{2,1,0:T(8,128)(2,1)}, u32[]{:S(2)}) copy-start(bf16[9,384,384]{2,1,0:T(8,128)(2,1)} %all-gather.3.cloned.1.call-done) | copy-start | bytes 7962628
  38.1 4.4 %copy-start.2 = (bf16[24,20,384]{2,1,0:T(8,128)(2,1)S(1)}, bf16[24,20,384]{2,1,0:T(8,128)(2,1)}, u32[]{:S(2)}) copy-start(bf16[24,20,384]{2,1,0:T(8,128)(2,1)} %get-tuple-element.12) | copy-start | bytes 1105924
  42.2 1.2 copy-start.5
  43.8 6.1 %collective-permute-start.4 = (bf16[16,16,384]{2,1,0:T(8,128)(2,1)S(1)}, bf16[16,16,384]{2,1,0:T(8,128)(2,1)S(1)}, u32[]{:S(2)}, u32[]{:S(2)}) collective-permute-start(bf16[16,16,384]{2,1,0:T(8,128)(2,1)S(1)} %get-tuple-element.19), channel_id=1, source_target_pairs={{0,8},{8,16},{16,24},{24,32},{32,40},{40,48},{48,56},{56,64},{64,7... | collective-permute-start | bytes 589832 | tf_op jit(solution)/shard_map/ppermute | solution.py:18
  45.9 8.0 %collective-permute-start.5 = (bf16[16,16,384]{2,1,0:T(8,128)(2,1)S(1)}, bf16[16,16,384]{2,1,0:T(8,128)(2,1)}, u32[]{:S(2)}, u32[]{:S(2)}) collective-permute-start(bf16[16,16,384]{2,1,0:T(8,128)(2,1)S(1)} %get-tuple-element.19), channel_id=1, source_target_pairs={{8,0},{16,8},{24,16},{32,24},{40,32},{48,40},{56,48},{64,56},{72,6... | collective-permute-start | bytes 589832 | tf_op jit(solution)/shard_map/ppermute | solution.py:20
  55.7 17.1 %collective-permute-start.6 = (bf16[48,16,384]{2,1,0:T(8,128)(2,1)}, bf16[48,16,384]{2,1,0:T(8,128)(2,1)}, u32[]{:S(2)}, u32[]{:S(2)}) collective-permute-start(bf16[48,16,384]{2,1,0:T(8,128)(2,1)} %pad_maximum_fusion), channel_id=1, source_target_pairs={{0,1},{1,2},{2,3},{3,4},{4,5},{5,6},{6,7},{8,9},{9,10},{10,11},{11... | collective-permute-start | bytes 1769480 | tf_op jit(solution)/shard_map/ppermute | solution.py:18
  67.6 6.6 %copy-start = (bf16[9,384,384]{2,1,0:T(8,128)(2,1)S(1)}, bf16[9,384,384]{2,1,0:T(8,128)(2,1)}, u32[]{:S(2)}) copy-start(bf16[9,384,384]{2,1,0:T(8,128)(2,1)} %all-gather.5.cloned.1.call-done) | copy-start | bytes 7962628
  69.0 16.8 %collective-permute-start.7 = (bf16[48,16,384]{2,1,0:T(8,128)(2,1)}, bf16[48,16,384]{2,1,0:T(8,128)(2,1)S(1)}, u32[]{:S(2)}, u32[]{:S(2)}) collective-permute-start(bf16[48,16,384]{2,1,0:T(8,128)(2,1)} %pad_maximum_fusion), channel_id=1, source_target_pairs={{1,0},{2,1},{3,2},{4,3},{5,4},{6,5},{7,6},{9,8},{10,9},{11,10},{12... | collective-permute-start | bytes 1769480 | tf_op jit(solution)/shard_map/ppermute | solution.py:20
  74.2 13.3 %copy-start.4 = (bf16[16,16,384]{2,1,0:T(8,128)(2,1)S(1)}, bf16[16,16,384]{2,1,0:T(8,128)(2,1)}, u32[]{:S(2)}) copy-start(bf16[16,16,384]{2,1,0:T(8,128)(2,1)} %param.9) | copy-start | bytes 589828
  74.2 13.3 %copy-start.6 = (f32[384]{0:T(512)S(1)}, f32[384]{0:T(512)}, u32[]{:S(2)}) copy-start(f32[384]{0:T(512)} %param.13) | copy-start | bytes 4612
  88.1 5.3 %collective-permute-start.8 = (bf16[16,16,384]{2,1,0:T(8,128)(2,1)S(1)}, bf16[16,16,384]{2,1,0:T(8,128)(2,1)S(1)}, u32[]{:S(2)}, u32[]{:S(2)}) collective-permute-start(bf16[16,16,384]{2,1,0:T(8,128)(2,1)S(1)} %fusion.42), channel_id=1, source_target_pairs={{0,8},{8,16},{16,24},{24,32},{32,40},{40,48},{48,56},{56,64},{64,7... | collective-permute-start | bytes 589832 | tf_op jit(solution)/shard_map/ppermute | solution.py:18
  90.2 7.0 %collective-permute-start.9 = (bf16[16,16,384]{2,1,0:T(8,128)(2,1)S(1)}, bf16[16,16,384]{2,1,0:T(8,128)(2,1)S(1)}, u32[]{:S(2)}, u32[]{:S(2)}) collective-permute-start(bf16[16,16,384]{2,1,0:T(8,128)(2,1)S(1)} %fusion.42), channel_id=1, source_target_pairs={{8,0},{16,8},{24,16},{32,24},{40,32},{48,40},{56,48},{64,56},{72,6... | collective-permute-start | bytes 589832 | tf_op jit(solution)/shard_map/ppermute | solution.py:20
  97.3 14.6 %collective-permute-start.10 = (bf16[48,16,384]{2,1,0:T(8,128)(2,1)S(1)}, bf16[48,16,384]{2,1,0:T(8,128)(2,1)S(1)}, u32[]{:S(2)}, u32[]{:S(2)}) collective-permute-start(bf16[48,16,384]{2,1,0:T(8,128)(2,1)S(1)} %pad_maximum_fusion.1), channel_id=1, source_target_pairs={{1,0},{2,1},{3,2},{4,3},{5,4},{6,5},{7,6},{9,8},{10,9},{11,10},{12... | collective-permute-start | bytes 1769480 | tf_op jit(solution)/shard_map/ppermute | solution.py:20
  98.9 14.2 %collective-permute-start.11 = (bf16[48,16,384]{2,1,0:T(8,128)(2,1)S(1)}, bf16[48,16,384]{2,1,0:T(8,128)(2,1)S(1)}, u32[]{:S(2)}, u32[]{:S(2)}) collective-permute-start(bf16[48,16,384]{2,1,0:T(8,128)(2,1)S(1)} %pad_maximum_fusion.1), channel_id=1, source_target_pairs={{0,1},{1,2},{2,3},{3,4},{4,5},{5,6},{6,7},{8,9},{9,10},{10,11},{11... | collective-permute-start | bytes 1769480 | tf_op jit(solution)/shard_map/ppermute | solution.py:18
  114.5 5.6 %collective-permute-start.13 = (bf16[4,16,384]{2,1,0:T(8,128)(2,1)S(1)}, bf16[4,16,384]{2,1,0:T(8,128)(2,1)S(1)}, u32[]{:S(2)}, u32[]{:S(2)}) collective-permute-start(bf16[4,16,384]{2,1,0:T(8,128)(2,1)S(1)} %get-tuple-element.16), channel_id=1, source_target_pairs={{8,0},{16,8},{24,16},{32,24},{40,32},{48,40},{56,48},{64,56},{72,6... | collective-permute-start | bytes 147464 | tf_op jit(solution)/shard_map/ppermute | solution.py:20
  115.8 5.2 %collective-permute-start.12 = (bf16[4,16,384]{2,1,0:T(8,128)(2,1)S(1)}, bf16[4,16,384]{2,1,0:T(8,128)(2,1)S(1)}, u32[]{:S(2)}, u32[]{:S(2)}) collective-permute-start(bf16[4,16,384]{2,1,0:T(8,128)(2,1)S(1)} %get-tuple-element.15), channel_id=1, source_target_pairs={{0,8},{8,16},{16,24},{24,32},{32,40},{40,48},{48,56},{56,64},{64,7... | collective-permute-start | bytes 147464 | tf_op jit(solution)/shard_map/ppermute | solution.py:18
  121.0 6.6 %collective-permute-start.14 = (bf16[24,4,384]{2,1,0:T(4,128)(2,1)S(1)}, bf16[24,4,384]{2,1,0:T(4,128)(2,1)S(1)}, u32[]{:S(2)}, u32[]{:S(2)}) collective-permute-start(bf16[24,4,384]{2,1,0:T(4,128)(2,1)S(1)} %get-tuple-element.9), channel_id=1, source_target_pairs={{1,0},{2,1},{3,2},{4,3},{5,4},{6,5},{7,6},{9,8},{10,9},{11,10},{12... | collective-permute-start | bytes 221192 | tf_op jit(solution)/shard_map/ppermute | solution.py:20
  122.3 6.1 %collective-permute-start.15 = (bf16[24,4,384]{2,1,0:T(4,128)(2,1)S(1)}, bf16[24,4,384]{2,1,0:T(4,128)(2,1)S(1)}, u32[]{:S(2)}, u32[]{:S(2)}) collective-permute-start(bf16[24,4,384]{2,1,0:T(4,128)(2,1)S(1)} %get-tuple-element.10), channel_id=1, source_target_pairs={{0,1},{1,2},{2,3},{3,4},{4,5},{5,6},{6,7},{8,9},{9,10},{10,11},{11... | collective-permute-start | bytes 221192 | tf_op jit(solution)/shard_map/ppermute | solution.py:18
  129.9 113.0 %copy-start.3 = (f32[16,16,384]{2,1,0:T(8,128)S(1)}, f32[16,16,384]{2,1,0:T(8,128)}, u32[]{:S(2)}) copy-start(f32[16,16,384]{2,1,0:T(8,128)} %get-tuple-element.5) | copy-start | bytes 1179652
Sparse Core Ops, SparseCore 0:
  9.4 28.5 all-gather.2
  40.1 27.3 all-gather.4
  131.4 111.4 all-reduce.1
where the time goes:
time: 252 us; the launch traced here: 251 us
  waiting for transfers between devices  171 us (68%)
  starting transfers between devices  39 us (15%)
  matrix products  20.7 us (8%)
  between operations  13.6 us (5%)
  other arithmetic  6.68 us (3%)
    psum x1, waiting for transfers between devices, shards(): grad_whole = lax.psum(point_grad, 'path')  112 us
    ppermute x8, waiting for transfers between devices, padded_2(): lax.ppermute(head, axis, [((i + 1) % count, i) for i in range(ends)])  33.8 us
    ppermute x8, starting transfers between devices, padded_2(): lax.ppermute(tail, axis, [(i, (i + 1) % count) for i in range(ends)])  28.6 us
    dot_general x18, matrix products, stencil(): jnp.dot(window, weights[tap_index], preferred_element_type=jnp.float32)  14.4 us
    ppermute x8, starting transfers between devices, padded_2(): lax.ppermute(head, axis, [((i + 1) % count, i) for i in range(ends)])  10.3 us
    all_gather x1, waiting for transfers between devices, shards(): lax.all_gather(first_weight, 'path', axis=1, tiled=True)  10.1 us
    all_gather x1, waiting for transfers between devices, shards(): lax.all_gather(second_weight, 'path', axis=1, tiled=True)  7.83 us
    ppermute x8, waiting for transfers between devices, padded_2(): lax.ppermute(tail, axis, [(i, (i + 1) % count) for i in range(ends)])  6.82 us
  transfers between devices with their start and end apart: 19, of which 14 were waited for; matrix products, arithmetic and copies ran while one was open for 8% of the time, Pallas kernels for 0%

commit v1 on v0

v1 whole, which is shorter than its diff:
```python
import functools

import jax
import jax.numpy as jnp
import numpy as np
from jax import lax
from jax.experimental import pallas as pl
from jax.experimental.pallas import tpu as pltpu
from jax.sharding import PartitionSpec as P

MESH = pl.DeviceIdType.MESH
F32 = jnp.float32
BF16 = jnp.bfloat16
C = 384
T = 16


def one_hot(rows, cols, pairs):
    out = np.zeros((rows, cols), np.float32)
    for r, c in pairs:
        out[r, c] = 1.0
    return out


def moves():
    split = one_hot(256, 256, [
        ((4 * s + c) * 16 + 4 * k + q, (4 * k + c) * 16 + 4 * q + s)
        for s in range(4) for c in range(4) for k in range(4) for q in range(4)])
    edges = one_hot(128, 256, [(m, 4 * m) for m in range(64)] + [(64 + m, 4 * m + 3) for m in range(64)])
    minus, plus = [], []
    for m in range(-4, 68):
        for q in range(4):
            f = 4 * (m + 4) + q
            outer_l = 16 + m if 0 <= m < 64 else (4 * (m + 4) + 3 if m < 0 else 80 + 4 * (m - 64) + 3)
            outer_r = 16 + m if 0 <= m < 64 else (4 * (m + 4) if m < 0 else 80 + 4 * (m - 64))
            minus.append((f, f - 1 if q else 288 + outer_l))
            plus.append((f, f + 1 if q < 3 else 288 + outer_r))
    minus = one_hot(288, 384, minus)
    plus = one_hot(288, 384, plus)
    join = one_hot(128, 128, [
        ((4 * k + c) * 16 + 4 * q + s, (4 * s + c) * 8 + 4 * k + q)
        for s in range(4) for c in range(4) for k in range(2) for q in range(4)])
    return [jnp.asarray(v, BF16) for v in (split, edges, minus, plus, join)]


def dot(a, b):
    return lax.dot_general(a, b, (((1,), (0,)), ((), ())), preferred_element_type=F32)


def dot_t(a, b):
    return lax.dot_general(a, b, (((1,), (1,)), ((), ())), preferred_element_type=F32)


ROOT = 0.7978845608028654


def gelu_parts(x):
    square = x * x
    t = jnp.tanh(ROOT * (x + 0.044715 * (x * square)))
    half = 0.5 * (1.0 + t)
    slope = half + 0.5 * x * (1.0 - t * t) * (ROOT * (1.0 + 3 * 0.044715 * square))
    return x * half, slope


def kernel(obs_h, base_h, cot_h, w1_h, b1_ref, w2_h, b2_ref, split_ref, edges_ref, minus_ref, plus_ref, join_ref,
           out_ref,
           obs, base, cot, snd, w1, w2, x, ct, h, hl, hr, a, al, ar, f, nl, nr, ml, mr, pk, qs, pre, slope, adj,
           psum_in, back,
           ls, ws, wr, as_, ar_, es, er, ps, pr, os_, or_):
    p = lax.axis_index("path")
    lon = lax.axis_index("lon")
    lat = lax.axis_index("lat")
    me = lon % T
    zhi = lon // T
    far = (lon + T) % (2 * T)
    has_l = lat > 0
    has_r = lat < 7

    loads = [pltpu.make_async_copy(src, dst, ls.at[i]) for i, (src, dst) in enumerate(
        ((obs_h, obs), (base_h, base), (cot_h, cot)))]
    for copy in loads:
        copy.start()
    half = pl.ds(pl.multiple_of(p * 192, 64), 192)
    own_w = [pltpu.make_async_copy(src, dst.at[:, half, :], ls.at[3 + i]) for i, (src, dst) in enumerate(
        ((w1_h, w1), (w2_h, w2)))]
    for copy in own_w:
        copy.start()

    barrier = pltpu.get_barrier_semaphore()

    def greet(**where):
        pl.semaphore_signal(barrier, inc=1, device_id=where, device_id_type=MESH)

    for o in range(1, T):
        greet(lon=zhi * T + (me + o) % T)
    greet(lon=far)
    greet(path=1 - p)

    @pl.when(has_l)
    def _():
        greet(lat=lat - 1)

    @pl.when(has_r)
    def _():
        greet(lat=lat + 1)

    blank = jnp.zeros((16, C), BF16)
    side = jnp.where(zhi == 0, 0, 17)
    for ref in (x, f, h, hl, hr, a, al, ar):
        ref[side] = blank
    nside = jnp.where(zhi == 0, 0, 5)
    for ref in (nl, nr, ml, mr):
        ref[nside] = blank

    @pl.when(jnp.logical_not(has_l))
    def _():
        for ref in (hl, al, nl, ml):
            ref[...] = jnp.zeros(ref.shape, BF16)

    @pl.when(jnp.logical_not(has_r))
    def _():
        for ref in (hr, ar, nr, mr):
            ref[...] = jnp.zeros(ref.shape, BF16)

    for copy in loads:
        copy.wait()
    low = base[...].astype(F32)
    mix = (p.astype(F32) + 0.5) / 2
    field = (low + mix * (obs[...].astype(F32) - low)).astype(BF16)
    snd[0] = dot(split_ref[...], field.reshape(256, C)).astype(BF16).reshape(T, 16, C)
    snd[1] = dot(split_ref[...], cot[...].reshape(256, C)).astype(BF16).reshape(T, 16, C)

    pl.semaphore_wait(barrier, 17 + has_l.astype(jnp.int32) + has_r.astype(jnp.int32))

    def spread(which, dst, o):
        d = (me + o) % T
        return pltpu.make_async_remote_copy(
            src_ref=snd.at[which, d], dst_ref=dst, send_sem=as_.at[which, o], recv_sem=ar_.at[which, o],
            device_id={"lon": zhi * T + d}, device_id_type=MESH)

    for o in range(1, T):
        spread(0, x.at[1 + me], o).start()
    push_w = [pltpu.make_async_remote_copy(
        src_ref=src, dst_ref=dst.at[:, half, :], send_sem=ws.at[i], recv_sem=wr.at[i],
        device_id={"path": 1 - p}, device_id_type=MESH) for i, (src, dst) in enumerate(((w1_h, w1), (w2_h, w2)))]
    push_w[0].start()
    for o in range(1, T):
        spread(1, ct.at[me], o).start()
    push_w[1].start()
    x[1 + me] = snd[0, me]
    ct[me] = snd[1, me]

    fs = jnp.where(zhi == 0, 16, 1)
    fd = jnp.where(zhi == 0, 0, 17)
    fr = jnp.where(zhi == 0, 17, 0)
    nf = jnp.where(zhi == 0, 5, 0)

    def send(stage, slot, src, dst, **where):
        return pltpu.make_async_remote_copy(
            src_ref=src, dst_ref=dst, send_sem=es.at[stage, slot], recv_sem=er.at[stage, slot],
            device_id=where, device_id_type=MESH)

    def exchange(stage, main, left, right, left_src, right_src, body, edge):
        to_far = send(stage, 2, main.at[fs], main.at[fd], lon=far)
        to_far.start()
        from_far = send(stage, 2, main.at[fs], main.at[fr], lon=far)

        def right_going():
            return [send(stage, 0, right_src, left.at[body], lat=lat + 1),
                    send(stage, 3, main.at[fr], left.at[edge], lat=lat + 1)]

        def left_going():
            return [send(stage, 1, left_src, right.at[body], lat=lat - 1),
                    send(stage, 4, main.at[fr], right.at[edge], lat=lat - 1)]

        @pl.when(has_r)
        def _():
            right_going()[0].start()

        @pl.when(has_l)
        def _():
            left_going()[0].start()

        from_far.wait_recv()

        @pl.when(has_r)
        def _():
            right_going()[1].start()

        @pl.when(has_l)
        def _():
            left_going()[1].start()

        @pl.when(has_l)
        def _():
            for copy in right_going():
                copy.wait_recv()

        @pl.when(has_r)
        def _():
            for copy in left_going():
                copy.wait_recv()

        def finish():
            to_far.wait_send()

            @pl.when(has_r)
            def _():
                for copy in right_going():
                    copy.wait_send()

            @pl.when(has_l)
            def _():
                for copy in left_going():
                    copy.wait_send()

        return finish

    inner = pl.ds(1, 16)

    def near_exchange(stage, main, left, right):
        pk[stage] = dot(edges_ref[...], main[inner].reshape(256, C)).astype(BF16).reshape(8, 16, C)
        return exchange(stage, main, left, right, pk.at[stage, pl.ds(0, 4)], pk.at[stage, pl.ds(4, 4)],
                        pl.ds(1, 4), nf)

    def near_windows(main, left, right):
        whole = main[...].reshape(288, C)
        qs[1] = whole.astype(F32)
        for j, move, outer in ((0, minus_ref, left), (2, plus_ref, right)):
            qs[j] = dot(move[:, :288], whole) + dot(move[:, 288:], outer[...].reshape(96, C))

    def near_conv(weights, forward):
        total = jnp.zeros((256, C), F32)
        for i in (-1, 0, 1):
            for j in (-1, 0, 1):
                sign = 1 if forward else -1
                window = qs[1 + sign * j, pl.ds(16 + 4 * sign * i, 256), :].astype(BF16)
                total = total + (dot if forward else dot_t)(window, weights[3 * (i + 1) + j + 1])
        return total

    def far_conv(parts, weights, forward):
        total = jnp.zeros((256, C), F32)
        for i in (-1, 0, 1):
            for j in (-1, 0, 1):
                sign = 1 if forward else -1
                window = parts[1 + sign * j][pl.ds(1 + sign * i, 16)].reshape(256, C)
                total = total + (dot if forward else dot_t)(window, weights[3 * (i + 1) + j + 1])
        return total

    for o in range(1, T):
        s = (me + T - o) % T
        pltpu.make_async_remote_copy(
            src_ref=snd.at[0, 0], dst_ref=x.at[1 + s], send_sem=as_.at[0, o], recv_sem=ar_.at[0, o],
            device_id={"lon": zhi * T + s}, device_id_type=MESH).wait_recv()

    done = [near_exchange(0, x, nl, nr)]
    near_windows(x, nl, nr)
    own_w[0].wait()
    push_w[0].wait_recv()
    act, der = gelu_parts(near_conv(w1, True) + b1_ref[...])
    slope[...] = der
    h[inner] = (x[inner].reshape(256, C).astype(F32) + act).astype(BF16).reshape(16, 16, C)

    done.append(exchange(1, h, hl, hr, h.at[inner], h.at[inner], inner, fr))
    own_w[1].wait()
    push_w[1].wait_recv()
    for o in range(1, T):
        s = (me + T - o) % T
        pltpu.make_async_remote_copy(
            src_ref=snd.at[1, 0], dst_ref=ct.at[s], send_sem=as_.at[1, o], recv_sem=ar_.at[1, o],
            device_id={"lon": zhi * T + s}, device_id_type=MESH).wait_recv()
    up = ct[...].reshape(256, C).astype(F32)
    _, der = gelu_parts(far_conv((hl, h, hr), w2, True) + b2_ref[...])
    a[inner] = (der * up).astype(BF16).reshape(16, 16, C)

    done.append(exchange(2, a, al, ar, a.at[inner], a.at[inner], inner, fr))
    hidden_adj = ct[...].reshape(256, C).astype(F32) + far_conv((al, a, ar), w2, False)
    adj[...] = hidden_adj
    f[inner] = (slope[...] * hidden_adj).astype(BF16).reshape(16, 16, C)

    done.append(near_exchange(3, f, ml, mr))
    near_windows(f, ml, mr)
    grad = adj[...] + near_conv(w1, False)
    pre[...] = grad.reshape(16, 2, 8, C)

    swap = pltpu.make_async_remote_copy(
        src_ref=pre.at[:, 1 - p], dst_ref=psum_in, send_sem=ps, recv_sem=pr,
        device_id={"path": 1 - p}, device_id_type=MESH)
    swap.start()
    swap.wait()
    pre[:, p] = pre[:, p] + psum_in[...]

    def collect(o):
        d = (me + o) % T
        return pltpu.make_async_remote_copy(
            src_ref=pre.at[d, p], dst_ref=back.at[me], send_sem=os_.at[o], recv_sem=or_.at[o],
            device_id={"lon": zhi * T + d}, device_id_type=MESH)

    for o in range(1, T):
        collect(o).start()
    back[me] = pre[me, p]
    for finish in done:
        finish()
    for o in range(1, T):
        for which in (0, 1):
            spread(which, x.at[1 + me] if which == 0 else ct.at[me], o).wait_send()
    for copy in push_w:
        copy.wait_send()
    for o in range(1, T):
        s = (me + T - o) % T
        pltpu.make_async_remote_copy(
            src_ref=pre.at[0, 0], dst_ref=back.at[s], send_sem=os_.at[o], recv_sem=or_.at[o],
            device_id={"lon": zhi * T + s}, device_id_type=MESH).wait_recv()
    got = back[...].reshape(128, C)
    top = got.astype(BF16)
    rest = (got - top.astype(F32)).astype(BF16)
    total = dot(join_ref[...], top) + dot(join_ref[...], rest)
    rows = pl.ds(p * 8, 8)
    diff = obs[rows].astype(F32) - base[rows].astype(F32)
    out_ref[...] = (diff * total.reshape(8, 16, C) / 2).astype(BF16)
    for o in range(1, T):
        collect(o).wait_send()


def shards(observed, baseline, cotangent, first_weight, first_bias, second_weight, second_bias):
    hbm = pl.BlockSpec(memory_space=pl.ANY)
    vmem = pl.BlockSpec(memory_space=pltpu.VMEM)
    block = pltpu.VMEM((16, 16, C), BF16)
    ext = pltpu.VMEM((18, 16, C), BF16)
    edge = pltpu.VMEM((6, 16, C), BF16)
    dma = pltpu.SemaphoreType.DMA
    return pl.pallas_call(
        kernel,
        out_shape=jax.ShapeDtypeStruct((8, 16, C), BF16),
        in_specs=[hbm, hbm, hbm, hbm, vmem, hbm, vmem] + [vmem] * 5,
        out_specs=vmem,
        scratch_shapes=[
            block, block, block, pltpu.VMEM((2, 16, 16, C), BF16),
            pltpu.VMEM((9, C, C), BF16), pltpu.VMEM((9, C, C), BF16),
            ext, block, ext, ext, ext, ext, ext, ext, ext, edge, edge, edge, edge,
            pltpu.VMEM((4, 8, 16, C), BF16),
            pltpu.VMEM((3, 288, C), F32),
            pltpu.VMEM((16, 2, 8, C), F32),
            pltpu.VMEM((256, C), F32), pltpu.VMEM((256, C), F32),
            pltpu.VMEM((16, 8, C), F32), pltpu.VMEM((16, 8, C), F32),
            dma((5,)), dma((2,)), dma((2,)), dma((2, T)), dma((2, T)), dma((4, 5)), dma((4, 5)),
            dma, dma, dma((T,)), dma((T,)),
        ],
        compiler_params=pltpu.CompilerParams(collective_id=0, has_side_effects=True),
    )(observed, baseline, cotangent, first_weight, first_bias.reshape(1, C), second_weight,
      second_bias.reshape(1, C), *moves())


def solution(mesh):
    placed = (
        P("lon", "lat", None),
        P("lon", "lat", None),
        P("lon", "lat", None),
        P(None, "path", None),
        P(),
        P(None, "path", None),
        P(),
    )
    return jax.shard_map(
        shards,
        mesh=mesh,
        in_specs=placed,
        out_specs=P(("lon", "path"), "lat", None),
        check_vma=False,
    )
```

time: 252 us -> 85.2 us (0.34)
  waiting for transfers between devices: 171 us -> 0 us
  Pallas kernels: 0 us -> 80.7 us
  starting transfers between devices: 39 us -> 0 us
  matrix products: 20.7 us -> 0 us
  between operations: 13.6 us -> 0.01 us
  other arithmetic: 6.68 us -> 0 us
  local copies, waits for them, and re-layouts: 0.06 us -> 4.06 us
    psum x1 -> x0, waiting for transfers between devices: 112 us -> none  [shards(): grad_whole = lax.psum(point_grad, 'path')]
    pallas_call x0 -> x1, Pallas kernels: none -> 80.7 us  [shards(): pl.pallas_call(kernel, out_shape=jax.ShapeDtypeStruct((8, 16, C), BF16),...]
    ppermute x16 -> x0, waiting for transfers between devices: 40.7 us -> none  [the longest x8 33.8 us: padded_2(): lax.ppermute(head, axis, [((i + 1) % count, i) for i in range(ends)])]
    ppermute x16 -> x0, starting transfers between devices: 38.9 us -> none  [the longest x8 28.6 us: padded_2(): lax.ppermute(tail, axis, [(i, (i + 1) % count) for i in range(ends)])]
    dot_general x36 -> x0, matrix products: 20.7 us -> none  [the longest x18 14.4 us: stencil(): jnp.dot(window, weights[tap_index], preferred_element_type=jnp.float32)]
    all_gather x2 -> x0, waiting for transfers between devices: 18 us -> none  [the longest x1 10.1 us: shards(): lax.all_gather(first_weight, 'path', axis=1, tiled=True)]
    concatenate x4 -> x0, other arithmetic: 3.13 us -> none  [padded_2(): jnp.concatenate([lax.ppermute(tail, axis, [(i, (i + 1) % count) for i in...]
    reshape x0 -> x2, local copies, waits for them, and re-layouts: none -> 2.52 us  [the longest x1 1.28 us: shards(): second_bias.reshape(1, C)]
  transfers between devices with their start and end apart: 19 -> 0, of which waited for: 14 -> 0; matrix products, arithmetic and copies ran while one was open for 8% -> 0% of each run, Pallas kernels for 0% -> 0%
where the time goes in v1:
time: 85.2 us; the launch traced here: 84.7 us
  Pallas kernels  80.7 us (95%)
  local copies, waits for them, and re-layouts  4.06 us (5%)
    pallas_call x1, Pallas kernels, shards(): pl.pallas_call(kernel, out_shape=jax.ShapeDtypeStruct((8, 16, C), BF16),...  80.7 us

profile of v1, /device:TPU:1, one launch (start us, length us, event | category | flops | bytes accessed | tf_op | source)
XLA Modules:
  0.0 84.7 jit_solution(10550767457446478168)
XLA Ops:
  0.0 1.2 %reshape.6.b1_ref = f32[1,384]{1,0:T(1,128)} reshape(f32[384]{0:T(512)} %param.16) | data formatting | bytes 3072 | tf_op jit(solution)/shard_map/reshape | solution.py:350
  1.2 1.3 %reshape.7.b2_ref = f32[1,384]{1,0:T(1,128)} reshape(f32[384]{0:T(512)} %param.18) | data formatting | bytes 3072 | tf_op jit(solution)/shard_map/reshape | solution.py:351
  2.5 80.7 %shard_map.118 = bf16[8,16,384]{2,1,0:T(8,128)(2,1)} custom-call(bf16[16,16,384]{2,1,0:T(8,128)(2,1)} %obs_h.1, bf16[16,16,384]{2,1,0:T(8,128)(2,1)} %base_h.1, bf16[16,16,384]{2,1,0:T(8,128)(2,1)} %cot_h.1, bf16[9,192,384]{2,1,0:T(8,128)(2,1)} %w1_h.1, f32[1,384]{1,0:T(1,128)} %reshape.6.b1_ref, bf16[9,192,384]{2,1,0:T(8,128)(2,1)} %w2_h.1, ...), custom_call_target="tpu_custom_call" | custom-call | tf_op jit(solution)/shard_map/pallas_call | solution.py:332
  83.2 1.5 %copy.14 = bf16[8,16,384]{2,1,0:T(8,128)(2,1)} copy(bf16[8,16,384]{2,1,0:T(8,128)(2,1)} %shard_map.118) | data formatting | bytes 196608

commit v2 on v1

v2 whole, which is shorter than its diff:
```python
import functools

import jax
import jax.numpy as jnp
import numpy as np
from jax import lax
from jax.experimental import pallas as pl
from jax.experimental.pallas import tpu as pltpu
from jax.sharding import PartitionSpec as P

MESH = pl.DeviceIdType.MESH
F32 = jnp.float32
BF16 = jnp.bfloat16
C = 384
T = 16


def one_hot(rows, cols, pairs):
    out = np.zeros((rows, cols), np.float32)
    for r, c in pairs:
        out[r, c] = 1.0
    return out


def moves():
    split = one_hot(256, 256, [
        ((4 * s + c) * 16 + 4 * k + q, (4 * k + c) * 16 + 4 * q + s)
        for s in range(4) for c in range(4) for k in range(4) for q in range(4)])
    edges = one_hot(128, 256, [(m, 4 * m) for m in range(64)] + [(64 + m, 4 * m + 3) for m in range(64)])
    edges_far = one_hot(32, 48, [(m, 4 * m) for m in range(12)] + [(16 + m, 4 * m + 3) for m in range(12)])

    def shift(rows, total, step):
        edge = 0 if step < 0 else 3
        return one_hot(4 * rows, total, [
            (4 * m + q, 4 * rows + m if q == edge else 4 * m + q + step) for m in range(rows) for q in range(4)])

    join = one_hot(128, 128, [
        ((4 * k + c) * 16 + 4 * q + s, (4 * s + c) * 8 + 4 * k + q)
        for s in range(4) for c in range(4) for k in range(2) for q in range(4)])
    return [jnp.asarray(v, BF16) for v in (
        split, edges, edges_far, shift(64, 320, -1), shift(64, 320, 1), shift(12, 64, -1), shift(12, 64, 1), join)]


def dot(a, b):
    return lax.dot_general(a, b, (((1,), (0,)), ((), ())), preferred_element_type=F32)


def dot_t(a, b):
    return lax.dot_general(a, b, (((1,), (1,)), ((), ())), preferred_element_type=F32)


ROOT = 0.7978845608028654


def gelu_parts(x):
    square = x * x
    t = jnp.tanh(ROOT * (x + 0.044715 * (x * square)))
    half = 0.5 * (1.0 + t)
    slope = half + 0.5 * x * (1.0 - t * t) * (ROOT * (1.0 + 3 * 0.044715 * square))
    return x * half, slope


def kernel(obs_h, base_h, cot_h, w1_h, b1_ref, w2_h, b2_ref, split_ref, edges_ref, edges_far_ref,
           minus_ref, plus_ref, minus_far_ref, plus_far_ref, join_ref,
           out_ref,
           obs, base, cot, snd, w1, w2, x, ct, h, hl, hr, a, al, ar, f, nl, nr, ml, mr, pk, pkf, hop, hop_ct,
           qs, qf, slope, adj, pre, psum_in, back,
           ls, ws, wr, as_, ar_, es, er, fs, fr, ps, pr, os_, or_):
    p = lax.axis_index("path")
    lon = lax.axis_index("lon")
    lat = lax.axis_index("lat")
    me = lon % T
    zhi = lon // T
    z = zhi * 8 + lat
    has_l = lat > 0
    has_r = lat < 7

    def along(step):
        there = (z + step + 16) % 16
        return {"lon": (there // 8) * T + me, "lat": there % 8}

    loads = [pltpu.make_async_copy(src, dst, ls.at[i]) for i, (src, dst) in enumerate(
        ((obs_h, obs), (base_h, base), (cot_h, cot)))]
    for copy in loads:
        copy.start()
    half = pl.ds(pl.multiple_of(p * 192, 64), 192)
    own_w = [pltpu.make_async_copy(src, dst.at[:, half, :], ls.at[3 + i]) for i, (src, dst) in enumerate(
        ((w1_h, w1), (w2_h, w2)))]
    for copy in own_w:
        copy.start()

    barrier = pltpu.get_barrier_semaphore()

    def greet(**where):
        pl.semaphore_signal(barrier, inc=1, device_id=where, device_id_type=MESH)

    for o in range(1, T):
        greet(lon=zhi * T + (me + o) % T)
    greet(path=1 - p)
    greet(**along(4))
    greet(**along(-4))

    @pl.when(has_l)
    def _():
        greet(lat=lat - 1)

    @pl.when(has_r)
    def _():
        greet(lat=lat + 1)

    outside = 2 + 17 * zhi
    past = 19 * (1 - zhi)
    blank = jnp.zeros((16, C), BF16)
    for ref in (h, hl, hr, a, al, ar):
        ref[outside] = blank
    for ref in (nl, nr, ml, mr):
        ref[0] = blank
        ref[5] = blank
    for t in (0, 1, 2, 19, 20, 21):
        f[t] = blank
    for j in range(3):
        qs[j, :64] = jnp.zeros((64, C), F32)
        qs[j, 320:] = jnp.zeros((64, C), F32)

    @pl.when(jnp.logical_not(has_l))
    def _():
        for ref in (hl, al, nl, ml):
            ref[...] = jnp.zeros(ref.shape, BF16)

    @pl.when(jnp.logical_not(has_r))
    def _():
        for ref in (hr, ar, nr, mr):
            ref[...] = jnp.zeros(ref.shape, BF16)

    for copy in loads:
        copy.wait()
    low = base[...].astype(F32)
    mix = (p.astype(F32) + 0.5) / 2
    field = (low + mix * (obs[...].astype(F32) - low)).astype(BF16)
    snd[0] = dot(split_ref[...], field.reshape(256, C)).astype(BF16).reshape(T, 16, C)
    snd[1] = dot(split_ref[...], cot[...].reshape(256, C)).astype(BF16).reshape(T, 16, C)

    pl.semaphore_wait(barrier, 18 + has_l.astype(jnp.int32) + has_r.astype(jnp.int32))

    def remote(src, dst, send_sem, recv_sem, where):
        return pltpu.make_async_remote_copy(
            src_ref=src, dst_ref=dst, send_sem=send_sem, recv_sem=recv_sem, device_id=where, device_id_type=MESH)

    def spread(which, o):
        d = (me + o) % T
        dst = (x, ct)[which].at[3 + me]
        return remote(snd.at[which, d], dst, as_.at[which, o], ar_.at[which, o], {"lon": zhi * T + d})

    def gathered(which, o):
        s = (me + T - o) % T
        dst = (x, ct)[which].at[3 + s]
        return remote(snd.at[which, s], dst, as_.at[which, o], ar_.at[which, o], {"lon": zhi * T + s})

    for o in range(1, T):
        spread(0, o).start()
    push_w = [remote(src, dst.at[:, half, :], ws.at[i], wr.at[i], {"path": 1 - p})
              for i, (src, dst) in enumerate(((w1_h, w1), (w2_h, w2)))]
    push_w[0].start()
    for o in range(1, T):
        spread(1, o).start()
    push_w[1].start()
    x[3 + me] = snd[0, me]
    ct[3 + me] = snd[1, me]

    def first_hop(slot):
        base_x, base_c = 16 - 13 * zhi, 17 - 14 * zhi
        src = (x.at[pl.ds(base_x, 2)], x.at[pl.ds(base_x + 2, 1)],
               ct.at[pl.ds(base_c, 1)], ct.at[pl.ds(base_c + 1, 1)])[slot]
        dst = (hop.at[pl.ds(0, 2)], hop.at[pl.ds(2, 1)], hop_ct.at[pl.ds(0, 1)], hop_ct.at[pl.ds(1, 1)])[slot]
        return remote(src, dst, fs.at[slot], fr.at[slot], along(-4 if slot % 2 else 4))

    def second_hop(slot, coming):
        if coming:
            side = 1 - zhi
        else:
            side = ((z + (4 if slot % 2 else -4) + 16) % 16) // 8
        base_x, base_c = 19 * side, 1 + 18 * side
        src = (hop.at[pl.ds(0, 2)], hop.at[pl.ds(2, 1)], hop_ct.at[pl.ds(0, 1)], hop_ct.at[pl.ds(1, 1)])[slot]
        dst = (x.at[pl.ds(base_x, 2)], x.at[pl.ds(base_x + 2, 1)],
               ct.at[pl.ds(base_c, 1)], ct.at[pl.ds(base_c + 1, 1)])[slot]
        return remote(src, dst, fs.at[4 + slot], fr.at[4 + slot], along(-4 if slot % 2 else 4))

    def right_going(stage, src, dst):
        return remote(src, dst, es.at[stage, 0], er.at[stage, 0], {"lat": lat + 1})

    def left_going(stage, src, dst):
        return remote(src, dst, es.at[stage, 1], er.at[stage, 1], {"lat": lat - 1})

    sent = []

    def give(stage, left_src, right_src, at_left, at_right):
        @pl.when(has_r)
        def _():
            right_going(stage, right_src, at_left).start()

        @pl.when(has_l)
        def _():
            left_going(stage, left_src, at_right).start()

        sent.append((stage, left_src, right_src, at_left, at_right))

    def take(stage):
        left_src, right_src, at_left, at_right = next(v[1:] for v in sent if v[0] == stage)

        @pl.when(has_l)
        def _():
            right_going(stage, right_src, at_left).wait_recv()

        @pl.when(has_r)
        def _():
            left_going(stage, left_src, at_right).wait_recv()

    def give_block(stage, main, left, right, start, count):
        window = pl.ds(start, count)
        give(stage, main.at[window], main.at[window], left.at[window], right.at[window])

    inner = pl.ds(3, 16)
    beyond = pl.ds(past, 3)
    edge = 5 * (1 - zhi)

    def give_edges(stage, main, left, right, layer):
        pk[layer] = dot(edges_ref[...], main[inner].reshape(256, C)).astype(BF16).reshape(8, 16, C)
        give(stage, pk.at[layer, pl.ds(0, 4)], pk.at[layer, pl.ds(4, 4)], left.at[pl.ds(1, 4)], right.at[pl.ds(1, 4)])

    def give_far_edges(stage, main, left, right, layer):
        pkf[layer] = dot(edges_far_ref[...], main[beyond].reshape(48, C)).astype(BF16).reshape(2, 16, C)
        give(stage, pkf.at[layer, pl.ds(0, 1)], pkf.at[layer, pl.ds(1, 1)],
             left.at[pl.ds(edge, 1)], right.at[pl.ds(edge, 1)])

    far_rows = pl.ds(pl.multiple_of(16 * (1 + past), 16), 48)

    def centre(main):
        qs[1, 64:320] = main[inner].reshape(256, C).astype(F32)

    def centre_far(main):
        qs[1, far_rows] = main[beyond].reshape(48, C).astype(F32)

    def sides(main, left, right):
        whole = main[inner].reshape(256, C)
        for j, move, outer in ((0, minus_ref, left), (2, plus_ref, right)):
            qs[j, 64:320] = dot(move[:, :256], whole) + dot(move[:, 256:], outer[pl.ds(1, 4)].reshape(64, C))

    def sides_far(main, left, right):
        whole = main[beyond].reshape(48, C)
        for j, move, outer in ((0, minus_far_ref, left), (2, plus_far_ref, right)):
            qs[j, far_rows] = dot(move[:, :48], whole) + dot(move[:, 48:], outer[edge])

    def near_conv(ref, first, rows, weights, forward, columns):
        total = jnp.zeros((rows, C), F32)
        sign = 1 if forward else -1
        for j in columns:
            for i in (-1, 0, 1):
                window = ref[1 + sign * j, pl.ds(first + 4 * sign * i, rows), :].astype(BF16)
                total = total + (dot if forward else dot_t)(window, weights[3 * (i + 1) + j + 1])
        return total

    def far_conv(parts, start, count, weights, forward):
        total = jnp.zeros((16 * count, C), F32)
        sign = 1 if forward else -1
        for j in (0, -1, 1):
            for i in (-1, 0, 1):
                window = parts[1 + sign * j][pl.ds(start + sign * i, count)].reshape(16 * count, C)
                total = total + (dot if forward else dot_t)(window, weights[3 * (i + 1) + j + 1])
        return total

    for o in range(1, T):
        gathered(0, o).wait_recv()

    first_hop(0).start()
    first_hop(1).start()
    give_edges(0, x, nl, nr, 0)
    centre(x)
    own_w[0].wait()
    push_w[0].wait_recv()
    total = near_conv(qs, 64, 256, w1, True, (0,))
    take(0)
    sides(x, nl, nr)
    act, der = gelu_parts(total + near_conv(qs, 64, 256, w1, True, (-1, 1)) + b1_ref[...])
    slope[inner] = der.reshape(16, 16, C)
    h[inner] = (x[inner].reshape(256, C).astype(F32) + act).astype(BF16).reshape(16, 16, C)
    give_block(2, h, hl, hr, 3 + zhi, 15)

    for slot in (0, 1):
        first_hop(slot).wait_recv()
        second_hop(slot, False).start()
    for o in range(1, T):
        gathered(1, o).wait_recv()
    first_hop(2).start()
    first_hop(3).start()
    own_w[1].wait()
    push_w[1].wait_recv()
    second_hop(0, True).wait_recv()
    second_hop(1, True).wait_recv()
    give_far_edges(1, x, nl, nr, 0)
    for slot in (2, 3):
        first_hop(slot).wait_recv()
        second_hop(slot, False).start()

    def second_forward(start, count):
        window = pl.ds(start, count)
        _, der = gelu_parts(far_conv((hl, h, hr), start, count, w2, True) + b2_ref[...])
        a[window] = (der * ct[window].reshape(16 * count, C).astype(F32)).astype(BF16).reshape(count, 16, C)

    take(2)
    early = 3 + 2 * zhi
    second_forward(early, 14)
    give_block(4, a, al, ar, early, 14)

    take(1)
    centre_far(x)
    sides_far(x, nl, nr)
    late = 18 * (1 - zhi)
    for j in range(3):
        qf[j] = qs[j, pl.ds(pl.multiple_of(16 * late, 16), 96)]
    act, der = gelu_parts(near_conv(qf, 16, 64, w1, True, (-1, 0, 1)) + b1_ref[...])
    window = pl.ds(late, 4)
    slope[window] = der.reshape(4, 16, C)
    h[window] = (x[window].reshape(64, C).astype(F32) + act).astype(BF16).reshape(4, 16, C)
    give_block(3, h, hl, hr, late, 4)
    second_hop(2, True).wait_recv()
    second_hop(3, True).wait_recv()
    take(3)
    late = 17 - 16 * zhi
    second_forward(late, 4)
    give_block(5, a, al, ar, late, 4)

    def second_adjoint(start, count):
        window = pl.ds(start, count)
        hidden_adj = ct[window].reshape(16 * count, C).astype(F32) + far_conv((al, a, ar), start, count, w2, False)
        adj[window] = hidden_adj.reshape(count, 16, C)
        f[window] = (slope[window].reshape(16 * count, C) * hidden_adj).astype(BF16).reshape(count, 16, C)

    take(4)
    second_adjoint(3 + 3 * zhi, 13)
    take(5)
    second_adjoint(16 - 14 * zhi, 4)

    give_edges(6, f, ml, mr, 1)
    give_far_edges(7, f, ml, mr, 1)
    centre(f)
    centre_far(f)
    total = adj[inner].reshape(256, C) + near_conv(qs, 64, 256, w1, False, (0,))
    take(6)
    take(7)
    sides(f, ml, mr)
    sides_far(f, ml, mr)
    total = total + near_conv(qs, 64, 256, w1, False, (-1, 1))
    pre[...] = total.reshape(16, 2, 8, C)

    swap = remote(pre.at[:, 1 - p], psum_in, ps, pr, {"path": 1 - p})
    swap.start()
    swap.wait()
    pre[:, p] = pre[:, p] + psum_in[...]

    def collect(o):
        d = (me + o) % T
        return remote(pre.at[d, p], back.at[me], os_.at[o], or_.at[o], {"lon": zhi * T + d})

    def collected(o):
        s = (me + T - o) % T
        return remote(pre.at[s, p], back.at[s], os_.at[o], or_.at[o], {"lon": zhi * T + s})

    for o in range(1, T):
        collect(o).start()
    back[me] = pre[me, p]
    for stage, left_src, right_src, at_left, at_right in sent:
        @pl.when(has_r)
        def _():
            right_going(stage, right_src, at_left).wait_send()

        @pl.when(has_l)
        def _():
            left_going(stage, left_src, at_right).wait_send()

    for slot in range(4):
        first_hop(slot).wait_send()
        second_hop(slot, False).wait_send()
    for o in range(1, T):
        for which in (0, 1):
            spread(which, o).wait_send()
    for copy in push_w:
        copy.wait_send()
    for o in range(1, T):
        collected(o).wait_recv()
    got = back[...].reshape(128, C)
    top = got.astype(BF16)
    rest = (got - top.astype(F32)).astype(BF16)
    total = dot(join_ref[...], top) + dot(join_ref[...], rest)
    rows = pl.ds(p * 8, 8)
    diff = obs[rows].astype(F32) - base[rows].astype(F32)
    out_ref[...] = (diff * total.reshape(8, 16, C) / 2).astype(BF16)
    for o in range(1, T):
        collect(o).wait_send()


def shards(observed, baseline, cotangent, first_weight, first_bias, second_weight, second_bias):
    hbm = pl.BlockSpec(memory_space=pl.ANY)
    vmem = pl.BlockSpec(memory_space=pltpu.VMEM)
    tiles = lambda n, dtype=BF16: pltpu.VMEM((n, 16, C), dtype)
    ext = tiles(22)
    dma = pltpu.SemaphoreType.DMA
    constants = moves()
    return pl.pallas_call(
        kernel,
        out_shape=jax.ShapeDtypeStruct((8, 16, C), BF16),
        in_specs=[hbm, hbm, hbm, hbm, vmem, hbm, vmem] + [vmem] * len(constants),
        out_specs=vmem,
        scratch_shapes=[
            tiles(16), tiles(16), tiles(16), pltpu.VMEM((2, 16, 16, C), BF16),
            pltpu.VMEM((9, C, C), BF16), pltpu.VMEM((9, C, C), BF16),
            ext, ext, ext, ext, ext, ext, ext, ext, ext, tiles(6), tiles(6), tiles(6), tiles(6),
            pltpu.VMEM((2, 8, 16, C), BF16), pltpu.VMEM((2, 2, 16, C), BF16), tiles(3), tiles(2),
            pltpu.VMEM((3, 384, C), F32), pltpu.VMEM((3, 96, C), F32),
            tiles(22, F32), tiles(22, F32),
            pltpu.VMEM((16, 2, 8, C), F32), pltpu.VMEM((16, 8, C), F32), pltpu.VMEM((16, 8, C), F32),
            dma((5,)), dma((2,)), dma((2,)), dma((2, T)), dma((2, T)), dma((8, 2)), dma((8, 2)), dma((8,)), dma((8,)),
            dma, dma, dma((T,)), dma((T,)),
        ],
        compiler_params=pltpu.CompilerParams(collective_id=0, has_side_effects=True),
    )(observed, baseline, cotangent, first_weight, first_bias.reshape(1, C), second_weight,
      second_bias.reshape(1, C), *constants)


def solution(mesh):
    placed = (
        P("lon", "lat", None),
        P("lon", "lat", None),
        P("lon", "lat", None),
        P(None, "path", None),
        P(),
        P(None, "path", None),
        P(),
    )
    return jax.shard_map(
        shards,
        mesh=mesh,
        in_specs=placed,
        out_specs=P(("lon", "path"), "lat", None),
        check_vma=False,
    )
```

time: 85.2 us -> 67.1 us (0.79)
  Pallas kernels: 80.7 us -> 62.3 us
    pallas_call x1, Pallas kernels: 80.7 us -> 62.3 us  [shards(): pl.pallas_call(kernel, out_shape=jax.ShapeDtypeStruct((8, 16, C), BF16),...]
where the time goes in v2:
time: 67.1 us; the launch traced here: 66.4 us
  Pallas kernels  62.3 us (93%)
  local copies, waits for them, and re-layouts  4.06 us (6%)
    pallas_call x1, Pallas kernels, shards(): pl.pallas_call(kernel, out_shape=jax.ShapeDtypeStruct((8, 16, C), BF16),...  62.3 us
    unnamed x1, local copies, waits for them, and re-layouts  1.54 us

profile of v2, /device:TPU:1, one launch (start us, length us, event | category | flops | bytes accessed | tf_op | source)
XLA Modules:
  0.0 66.4 jit_solution(8386184337532361800)
XLA Ops:
  0.0 1.2 %reshape.6.b1_ref = f32[1,384]{1,0:T(1,128)} reshape(f32[384]{0:T(512)} %param.19) | data formatting | bytes 3072 | tf_op jit(solution)/shard_map/reshape | solution.py:425
  1.2 1.3 %reshape.7.b2_ref = f32[1,384]{1,0:T(1,128)} reshape(f32[384]{0:T(512)} %param.21) | data formatting | bytes 3072 | tf_op jit(solution)/shard_map/reshape | solution.py:426
  2.5 62.3 %shard_map.145 = bf16[8,16,384]{2,1,0:T(8,128)(2,1)} custom-call(bf16[16,16,384]{2,1,0:T(8,128)(2,1)} %obs_h.1, bf16[16,16,384]{2,1,0:T(8,128)(2,1)} %base_h.1, bf16[16,16,384]{2,1,0:T(8,128)(2,1)} %cot_h.1, bf16[9,192,384]{2,1,0:T(8,128)(2,1)} %w1_h.1, f32[1,384]{1,0:T(1,128)} %reshape.6.b1_ref, bf16[9,192,384]{2,1,0:T(8,128)(2,1)} %w2_h.1, ...), custom_call_target="tpu_custom_call" | custom-call | tf_op jit(solution)/shard_map/pallas_call | solution.py:408
  64.9 1.5 %copy.17 = bf16[8,16,384]{2,1,0:T(8,128)(2,1)} copy(bf16[8,16,384]{2,1,0:T(8,128)(2,1)} %shard_map.145) | data formatting | bytes 196608

commit v3 on v2

--- a/solution.py
+++ b/solution.py
@@ -37,8 +37,8 @@
     join = one_hot(128, 128, [
         ((4 * k + c) * 16 + 4 * q + s, (4 * s + c) * 8 + 4 * k + q)
         for s in range(4) for c in range(4) for k in range(2) for q in range(4)])
-    return [jnp.asarray(v, BF16) for v in (
-        split, edges, edges_far, shift(64, 320, -1), shift(64, 320, 1), shift(12, 64, -1), shift(12, 64, 1), join)]
+    parts = (split, edges, edges_far, shift(64, 320, -1), shift(64, 320, 1), shift(12, 64, -1), shift(12, 64, 1), join)
+    return jnp.asarray(np.concatenate([np.pad(v, ((0, 0), (0, 384 - v.shape[1]))) for v in parts]), BF16)
 
 
 def dot(a, b):
@@ -60,10 +60,9 @@
     return x * half, slope
 
 
-def kernel(obs_h, base_h, cot_h, w1_h, b1_ref, w2_h, b2_ref, split_ref, edges_ref, edges_far_ref,
-           minus_ref, plus_ref, minus_far_ref, plus_far_ref, join_ref,
+def kernel(obs_h, base_h, cot_h, w1_h, b1_h, w2_h, b2_h, moves_h,
            out_ref,
-           obs, base, cot, snd, w1, w2, x, ct, h, hl, hr, a, al, ar, f, nl, nr, ml, mr, pk, pkf, hop, hop_ct,
+           table, b1_ref, b2_ref, obs, base, cot, snd, w1, w2, x, ct, h, hl, hr, a, al, ar, f, nl, nr, ml, mr, pk, pkf,
            qs, qf, slope, adj, pre, psum_in, back,
            ls, ws, wr, as_, ar_, es, er, fs, fr, ps, pr, os_, or_):
     p = lax.axis_index("path")
@@ -71,23 +70,18 @@
     lat = lax.axis_index("lat")
     me = lon % T
     zhi = lon // T
-    z = zhi * 8 + lat
     has_l = lat > 0
     has_r = lat < 7
 
-    def along(step):
-        there = (z + step + 16) % 16
-        return {"lon": (there // 8) * T + me, "lat": there % 8}
+    across = {"lon": (lon + T) % (2 * T)}
 
     loads = [pltpu.make_async_copy(src, dst, ls.at[i]) for i, (src, dst) in enumerate(
         ((obs_h, obs), (base_h, base), (cot_h, cot)))]
-    for copy in loads:
-        copy.start()
     half = pl.ds(pl.multiple_of(p * 192, 64), 192)
     own_w = [pltpu.make_async_copy(src, dst.at[:, half, :], ls.at[3 + i]) for i, (src, dst) in enumerate(
         ((w1_h, w1), (w2_h, w2)))]
-    for copy in own_w:
-        copy.start()
+    more = [pltpu.make_async_copy(src, dst, ls.at[5 + i]) for i, (src, dst) in enumerate(
+        ((moves_h, table), (b1_h, b1_ref), (b2_h, b2_ref)))]
 
     barrier = pltpu.get_barrier_semaphore()
 
@@ -97,8 +91,7 @@
     for o in range(1, T):
         greet(lon=zhi * T + (me + o) % T)
     greet(path=1 - p)
-    greet(**along(4))
-    greet(**along(-4))
+    greet(**across)
 
     @pl.when(has_l)
     def _():
@@ -107,6 +100,14 @@
     @pl.when(has_r)
     def _():
         greet(lat=lat + 1)
+
+    for copy in loads + more + own_w:
+        copy.start()
+
+    starts = np.cumsum([0, 256, 128, 32, 256, 256, 48, 48])
+    split_ref, edges_ref, edges_far_ref, minus_ref, plus_ref, minus_far_ref, plus_far_ref, join_ref = (
+        table.at[int(first):int(first) + size, :width] for first, size, width in zip(
+            starts, (256, 128, 32, 256, 256, 48, 48, 128), (256, 256, 48, 384, 384, 128, 128, 128)))
 
     outside = 2 + 17 * zhi
     past = 19 * (1 - zhi)
@@ -132,7 +133,7 @@
         for ref in (hr, ar, nr, mr):
             ref[...] = jnp.zeros(ref.shape, BF16)
 
-    for copy in loads:
+    for copy in loads + more:
         copy.wait()
     low = base[...].astype(F32)
     mix = (p.astype(F32) + 0.5) / 2
@@ -140,7 +141,7 @@
     snd[0] = dot(split_ref[...], field.reshape(256, C)).astype(BF16).reshape(T, 16, C)
     snd[1] = dot(split_ref[...], cot[...].reshape(256, C)).astype(BF16).reshape(T, 16, C)
 
-    pl.semaphore_wait(barrier, 18 + has_l.astype(jnp.int32) + has_r.astype(jnp.int32))
+    pl.semaphore_wait(barrier, 17 + has_l.astype(jnp.int32) + has_r.astype(jnp.int32))
 
     def remote(src, dst, send_sem, recv_sem, where):
         return pltpu.make_async_remote_copy(
@@ -167,23 +168,10 @@
     x[3 + me] = snd[0, me]
     ct[3 + me] = snd[1, me]
 
-    def first_hop(slot):
-        base_x, base_c = 16 - 13 * zhi, 17 - 14 * zhi
-        src = (x.at[pl.ds(base_x, 2)], x.at[pl.ds(base_x + 2, 1)],
-               ct.at[pl.ds(base_c, 1)], ct.at[pl.ds(base_c + 1, 1)])[slot]
-        dst = (hop.at[pl.ds(0, 2)], hop.at[pl.ds(2, 1)], hop_ct.at[pl.ds(0, 1)], hop_ct.at[pl.ds(1, 1)])[slot]
-        return remote(src, dst, fs.at[slot], fr.at[slot], along(-4 if slot % 2 else 4))
-
-    def second_hop(slot, coming):
-        if coming:
-            side = 1 - zhi
-        else:
-            side = ((z + (4 if slot % 2 else -4) + 16) % 16) // 8
-        base_x, base_c = 19 * side, 1 + 18 * side
-        src = (hop.at[pl.ds(0, 2)], hop.at[pl.ds(2, 1)], hop_ct.at[pl.ds(0, 1)], hop_ct.at[pl.ds(1, 1)])[slot]
-        dst = (x.at[pl.ds(base_x, 2)], x.at[pl.ds(base_x + 2, 1)],
-               ct.at[pl.ds(base_c, 1)], ct.at[pl.ds(base_c + 1, 1)])[slot]
-        return remote(src, dst, fs.at[4 + slot], fr.at[4 + slot], along(-4 if slot % 2 else 4))
+    def seam(slot, coming=False):
+        side = 1 - zhi if coming else zhi
+        ref, base, at, count = ((x, 16 - 13 * zhi, 19 * side, 3), (ct, 17 - 14 * zhi, 1 + 18 * side, 2))[slot]
+        return remote(ref.at[pl.ds(base, count)], ref.at[pl.ds(at, count)], fs.at[slot], fr.at[slot], across)
 
     def right_going(stage, src, dst):
         return remote(src, dst, es.at[stage, 0], er.at[stage, 0], {"lat": lat + 1})
@@ -243,12 +231,12 @@
     def sides(main, left, right):
         whole = main[inner].reshape(256, C)
         for j, move, outer in ((0, minus_ref, left), (2, plus_ref, right)):
-            qs[j, 64:320] = dot(move[:, :256], whole) + dot(move[:, 256:], outer[pl.ds(1, 4)].reshape(64, C))
+            qs[j, 64:320] = dot(move[:, :256], whole) + dot(move[:, 256:320], outer[pl.ds(1, 4)].reshape(64, C))
 
     def sides_far(main, left, right):
         whole = main[beyond].reshape(48, C)
         for j, move, outer in ((0, minus_far_ref, left), (2, plus_far_ref, right)):
-            qs[j, far_rows] = dot(move[:, :48], whole) + dot(move[:, 48:], outer[edge])
+            qs[j, far_rows] = dot(move[:, :48], whole) + dot(move[:, 48:64], outer[edge])
 
     def near_conv(ref, first, rows, weights, forward, columns):
         total = jnp.zeros((rows, C), F32)
@@ -271,8 +259,7 @@
     for o in range(1, T):
         gathered(0, o).wait_recv()
 
-    first_hop(0).start()
-    first_hop(1).start()
+    seam(0).start()
     give_edges(0, x, nl, nr, 0)
     centre(x)
     own_w[0].wait()
@@ -285,21 +272,13 @@
     h[inner] = (x[inner].reshape(256, C).astype(F32) + act).astype(BF16).reshape(16, 16, C)
     give_block(2, h, hl, hr, 3 + zhi, 15)
 
-    for slot in (0, 1):
-        first_hop(slot).wait_recv()
-        second_hop(slot, False).start()
     for o in range(1, T):
         gathered(1, o).wait_recv()
-    first_hop(2).start()
-    first_hop(3).start()
+    seam(1).start()
     own_w[1].wait()
     push_w[1].wait_recv()
-    second_hop(0, True).wait_recv()
-    second_hop(1, True).wait_recv()
+    seam(0, True).wait_recv()
     give_far_edges(1, x, nl, nr, 0)
-    for slot in (2, 3):
-        first_hop(slot).wait_recv()
-        second_hop(slot, False).start()
 
     def second_forward(start, count):
         window = pl.ds(start, count)
@@ -322,8 +301,7 @@
     slope[window] = der.reshape(4, 16, C)
     h[window] = (x[window].reshape(64, C).astype(F32) + act).astype(BF16).reshape(4, 16, C)
     give_block(3, h, hl, hr, late, 4)
-    second_hop(2, True).wait_recv()
-    second_hop(3, True).wait_recv()
+    seam(1, True).wait_recv()
     take(3)
     late = 17 - 16 * zhi
     second_forward(late, 4)
@@ -349,24 +327,31 @@
     take(7)
     sides(f, ml, mr)
     sides_far(f, ml, mr)
-    total = total + near_conv(qs, 64, 256, w1, False, (-1, 1))
     pre[...] = total.reshape(16, 2, 8, C)
 
-    swap = remote(pre.at[:, 1 - p], psum_in, ps, pr, {"path": 1 - p})
-    swap.start()
-    swap.wait()
-    pre[:, p] = pre[:, p] + psum_in[...]
-
-    def collect(o):
-        d = (me + o) % T
-        return remote(pre.at[d, p], back.at[me], os_.at[o], or_.at[o], {"lon": zhi * T + d})
-
-    def collected(o):
-        s = (me + T - o) % T
-        return remote(pre.at[s, p], back.at[s], os_.at[o], or_.at[o], {"lon": zhi * T + s})
-
-    for o in range(1, T):
-        collect(o).start()
+    def swap(part):
+        tiles = pl.ds(8 * part, 8)
+        return remote(pre.at[tiles, 1 - p], psum_in.at[tiles], ps.at[part], pr.at[part], {"path": 1 - p})
+
+    def collect(d):
+        return remote(pre.at[d, p], back.at[me], os_.at[d], or_.at[me], {"lon": zhi * T + d})
+
+    def collected(s):
+        return remote(pre.at[s, p], back.at[s], os_.at[s], or_.at[s], {"lon": zhi * T + s})
+
+    for part in (0, 1):
+        rest = near_conv(qs, 64 + 128 * part, 128, w1, False, (-1, 1))
+        tiles = pl.ds(8 * part, 8)
+        pre[tiles] = pre[tiles] + rest.reshape(8, 2, 8, C)
+        swap(part).start()
+    for part in (0, 1):
+        swap(part).wait()
+        tiles = pl.ds(8 * part, 8)
+        pre[tiles, p] = pre[tiles, p] + psum_in[tiles]
+        for d in range(8 * part, 8 * part + 8):
+            @pl.when(me != d)
+            def _():
+                collect(d).start()
     back[me] = pre[me, p]
     for stage, left_src, right_src, at_left, at_right in sent:
         @pl.when(has_r)
@@ -377,16 +362,15 @@
         def _():
             left_going(stage, left_src, at_right).wait_send()
 
-    for slot in range(4):
-        first_hop(slot).wait_send()
-        second_hop(slot, False).wait_send()
+    seam(0).wait_send()
+    seam(1).wait_send()
     for o in range(1, T):
         for which in (0, 1):
             spread(which, o).wait_send()
     for copy in push_w:
         copy.wait_send()
     for o in range(1, T):
-        collected(o).wait_recv()
+        collected((me + o) % T).wait_recv()
     got = back[...].reshape(128, C)
     top = got.astype(BF16)
     rest = (got - top.astype(F32)).astype(BF16)
@@ -395,7 +379,7 @@
     diff = obs[rows].astype(F32) - base[rows].astype(F32)
     out_ref[...] = (diff * total.reshape(8, 16, C) / 2).astype(BF16)
     for o in range(1, T):
-        collect(o).wait_send()
+        collect((me + o) % T).wait_send()
 
 
 def shards(observed, baseline, cotangent, first_weight, first_bias, second_weight, second_bias):
@@ -408,22 +392,23 @@
     return pl.pallas_call(
         kernel,
         out_shape=jax.ShapeDtypeStruct((8, 16, C), BF16),
-        in_specs=[hbm, hbm, hbm, hbm, vmem, hbm, vmem] + [vmem] * len(constants),
+        in_specs=[hbm] * 8,
         out_specs=vmem,
         scratch_shapes=[
+            pltpu.VMEM(constants.shape, BF16), pltpu.VMEM((1, C), F32), pltpu.VMEM((1, C), F32),
             tiles(16), tiles(16), tiles(16), pltpu.VMEM((2, 16, 16, C), BF16),
             pltpu.VMEM((9, C, C), BF16), pltpu.VMEM((9, C, C), BF16),
             ext, ext, ext, ext, ext, ext, ext, ext, ext, tiles(6), tiles(6), tiles(6), tiles(6),
-            pltpu.VMEM((2, 8, 16, C), BF16), pltpu.VMEM((2, 2, 16, C), BF16), tiles(3), tiles(2),
+            pltpu.VMEM((2, 8, 16, C), BF16), pltpu.VMEM((2, 2, 16, C), BF16),
             pltpu.VMEM((3, 384, C), F32), pltpu.VMEM((3, 96, C), F32),
             tiles(22, F32), tiles(22, F32),
             pltpu.VMEM((16, 2, 8, C), F32), pltpu.VMEM((16, 8, C), F32), pltpu.VMEM((16, 8, C), F32),
-            dma((5,)), dma((2,)), dma((2,)), dma((2, T)), dma((2, T)), dma((8, 2)), dma((8, 2)), dma((8,)), dma((8,)),
-            dma, dma, dma((T,)), dma((T,)),
+            dma((8,)), dma((2,)), dma((2,)), dma((2, T)), dma((2, T)), dma((8, 2)), dma((8, 2)), dma((2,)), dma((2,)),
+            dma((2,)), dma((2,)), dma((T,)), dma((T,)),
         ],
         compiler_params=pltpu.CompilerParams(collective_id=0, has_side_effects=True),
     )(observed, baseline, cotangent, first_weight, first_bias.reshape(1, C), second_weight,
-      second_bias.reshape(1, C), *constants)
+      second_bias.reshape(1, C), constants)
 
 
 def solution(mesh):

time: 67.1 us -> 66.1 us (0.985)
  no operation moved by 1% of the time
where the time goes in v3:
time: 66.1 us; the launch traced here: 65.9 us
  Pallas kernels  61.8 us (93%)
  local copies, waits for them, and re-layouts  4.06 us (6%)
    pallas_call x1, Pallas kernels, shards(): pl.pallas_call(kernel, out_shape=jax.ShapeDtypeStruct((8, 16, C), BF16),...  61.8 us
    unnamed x1, local copies, waits for them, and re-layouts  1.54 us

profile of v3, /device:TPU:1, one launch (start us, length us, event | category | flops | bytes accessed | tf_op | source)
XLA Modules:
  0.0 65.9 jit_solution(8866401002885122197)
XLA Ops:
  0.0 1.2 %reshape.6.b1_h = f32[1,384]{1,0:T(1,128)} reshape(f32[384]{0:T(512)} %param.12) | data formatting | bytes 3072 | tf_op jit(solution)/shard_map/reshape | solution.py:410
  1.2 1.3 %reshape.7.b2_h = f32[1,384]{1,0:T(1,128)} reshape(f32[384]{0:T(512)} %param.14) | data formatting | bytes 3072 | tf_op jit(solution)/shard_map/reshape | solution.py:411
  2.5 61.8 %shard_map.82 = bf16[8,16,384]{2,1,0:T(8,128)(2,1)} custom-call(bf16[16,16,384]{2,1,0:T(8,128)(2,1)} %obs_h.1, bf16[16,16,384]{2,1,0:T(8,128)(2,1)} %base_h.1, bf16[16,16,384]{2,1,0:T(8,128)(2,1)} %cot_h.1, bf16[9,192,384]{2,1,0:T(8,128)(2,1)} %w1_h.1, f32[1,384]{1,0:T(1,128)} %reshape.6.b1_h, bf16[9,192,384]{2,1,0:T(8,128)(2,1)} %w2_h.1, ...), custom_call_target="tpu_custom_call" | custom-call | tf_op jit(solution)/shard_map/pallas_call | solution.py:392
  64.4 1.5 %copy.10 = bf16[8,16,384]{2,1,0:T(8,128)(2,1)} copy(bf16[8,16,384]{2,1,0:T(8,128)(2,1)} %shard_map.82) | data formatting | bytes 196608

commit v4 on v3

--- a/solution.py
+++ b/solution.py
@@ -63,8 +63,8 @@
 def kernel(obs_h, base_h, cot_h, w1_h, b1_h, w2_h, b2_h, moves_h,
            out_ref,
            table, b1_ref, b2_ref, obs, base, cot, snd, w1, w2, x, ct, h, hl, hr, a, al, ar, f, nl, nr, ml, mr, pk, pkf,
-           qs, qf, slope, adj, pre, psum_in, back,
-           ls, ws, wr, as_, ar_, es, er, fs, fr, ps, pr, os_, or_):
+           qs, qf, slope, adj, pre, back,
+           ls, ws, wr, as_, ar_, es, er, fs, fr, os_, or_, near_up, near_down, mid_up, mid_down, wide_up, wide_down):
     p = lax.axis_index("path")
     lon = lax.axis_index("lon")
     lat = lax.axis_index("lat")
@@ -73,7 +73,12 @@
     has_l = lat > 0
     has_r = lat < 7
 
+    z = zhi * 8 + lat
     across = {"lon": (lon + T) % (2 * T)}
+
+    def along(step):
+        there = (z + step + 16) % 16
+        return {"lon": (there // 8) * T + me, "lat": there % 8}
 
     loads = [pltpu.make_async_copy(src, dst, ls.at[i]) for i, (src, dst) in enumerate(
         ((obs_h, obs), (base_h, base), (cot_h, cot)))]
@@ -91,15 +96,8 @@
     for o in range(1, T):
         greet(lon=zhi * T + (me + o) % T)
     greet(path=1 - p)
-    greet(**across)
-
-    @pl.when(has_l)
-    def _():
-        greet(lat=lat - 1)
-
-    @pl.when(has_r)
-    def _():
-        greet(lat=lat + 1)
+    greet(**along(1))
+    greet(**along(-1))
 
     for copy in loads + more + own_w:
         copy.start()
@@ -141,7 +139,7 @@
     snd[0] = dot(split_ref[...], field.reshape(256, C)).astype(BF16).reshape(T, 16, C)
     snd[1] = dot(split_ref[...], cot[...].reshape(256, C)).astype(BF16).reshape(T, 16, C)
 
-    pl.semaphore_wait(barrier, 17 + has_l.astype(jnp.int32) + has_r.astype(jnp.int32))
+    pl.semaphore_wait(barrier, 18)
 
     def remote(src, dst, send_sem, recv_sem, where):
         return pltpu.make_async_remote_copy(
@@ -167,6 +165,12 @@
     push_w[1].start()
     x[3 + me] = snd[0, me]
     ct[3 + me] = snd[1, me]
+
+    for step, up, down in ((1, near_up, near_down), (2, mid_up, mid_down), (4, wide_up, wide_down)):
+        pl.semaphore_signal(up, inc=1, device_id=along(step), device_id_type=MESH)
+        pl.semaphore_signal(down, inc=1, device_id=along(-step), device_id_type=MESH)
+        pl.semaphore_wait(up, 1)
+        pl.semaphore_wait(down, 1)
 
     def seam(slot, coming=False):
         side = 1 - zhi if coming else zhi
@@ -270,7 +274,8 @@
     act, der = gelu_parts(total + near_conv(qs, 64, 256, w1, True, (-1, 1)) + b1_ref[...])
     slope[inner] = der.reshape(16, 16, C)
     h[inner] = (x[inner].reshape(256, C).astype(F32) + act).astype(BF16).reshape(16, 16, C)
-    give_block(2, h, hl, hr, 3 + zhi, 15)
+    give_block(2, h, hl, hr, 3 + 8 * zhi, 8)
+    give_block(8, h, hl, hr, 11 - 7 * zhi, 7)
 
     for o in range(1, T):
         gathered(1, o).wait_recv()
@@ -286,9 +291,13 @@
         a[window] = (der * ct[window].reshape(16 * count, C).astype(F32)).astype(BF16).reshape(count, 16, C)
 
     take(2)
-    early = 3 + 2 * zhi
-    second_forward(early, 14)
-    give_block(4, a, al, ar, early, 14)
+    early = 3 + 9 * zhi
+    second_forward(early, 7)
+    give_block(4, a, al, ar, early, 7)
+    take(8)
+    early = 10 - 5 * zhi
+    second_forward(early, 7)
+    give_block(9, a, al, ar, early, 7)
 
     take(1)
     centre_far(x)
@@ -314,7 +323,9 @@
         f[window] = (slope[window].reshape(16 * count, C) * hidden_adj).astype(BF16).reshape(count, 16, C)
 
     take(4)
-    second_adjoint(3 + 3 * zhi, 13)
+    second_adjoint(3 + 10 * zhi, 6)
+    take(9)
+    second_adjoint(9 - 3 * zhi, 7)
     take(5)
     second_adjoint(16 - 14 * zhi, 4)
 
@@ -327,32 +338,23 @@
     take(7)
     sides(f, ml, mr)
     sides_far(f, ml, mr)
-    pre[...] = total.reshape(16, 2, 8, C)
-
-    def swap(part):
-        tiles = pl.ds(8 * part, 8)
-        return remote(pre.at[tiles, 1 - p], psum_in.at[tiles], ps.at[part], pr.at[part], {"path": 1 - p})
-
-    def collect(d):
-        return remote(pre.at[d, p], back.at[me], os_.at[d], or_.at[me], {"lon": zhi * T + d})
-
-    def collected(s):
-        return remote(pre.at[s, p], back.at[s], os_.at[s], or_.at[s], {"lon": zhi * T + s})
-
-    for part in (0, 1):
-        rest = near_conv(qs, 64 + 128 * part, 128, w1, False, (-1, 1))
-        tiles = pl.ds(8 * part, 8)
-        pre[tiles] = pre[tiles] + rest.reshape(8, 2, 8, C)
-        swap(part).start()
-    for part in (0, 1):
-        swap(part).wait()
-        tiles = pl.ds(8 * part, 8)
-        pre[tiles, p] = pre[tiles, p] + psum_in[tiles]
-        for d in range(8 * part, 8 * part + 8):
-            @pl.when(me != d)
-            def _():
-                collect(d).start()
-    back[me] = pre[me, p]
+    total = total + near_conv(qs, 64, 256, w1, False, (-1, 1))
+    pre[...] = total.reshape(16, 2, 8, C).astype(BF16)
+
+    def collect(o, core):
+        d = (me + o) % T
+        return remote(pre.at[d, core], back.at[p, me], os_.at[o, core], or_.at[o, p],
+                      {"lon": zhi * T + d, "path": core})
+
+    def collected(o, core):
+        s = (me + T - o) % T
+        return remote(pre.at[s, p], back.at[core, s], os_.at[o, core], or_.at[o, core],
+                      {"lon": zhi * T + s, "path": core})
+
+    for o in range(T):
+        for core in (p, 1 - p)[0 if o else 1:]:
+            collect(o, core).start()
+    back[p, me] = pre[me, p]
     for stage, left_src, right_src, at_left, at_right in sent:
         @pl.when(has_r)
         def _():
@@ -369,17 +371,16 @@
             spread(which, o).wait_send()
     for copy in push_w:
         copy.wait_send()
-    for o in range(1, T):
-        collected((me + o) % T).wait_recv()
-    got = back[...].reshape(128, C)
-    top = got.astype(BF16)
-    rest = (got - top.astype(F32)).astype(BF16)
-    total = dot(join_ref[...], top) + dot(join_ref[...], rest)
+    for o in range(T):
+        for core in (p, 1 - p)[0 if o else 1:]:
+            collected(o, core).wait_recv()
+    total = dot(join_ref[...], back[0].reshape(128, C)) + dot(join_ref[...], back[1].reshape(128, C))
     rows = pl.ds(p * 8, 8)
     diff = obs[rows].astype(F32) - base[rows].astype(F32)
     out_ref[...] = (diff * total.reshape(8, 16, C) / 2).astype(BF16)
-    for o in range(1, T):
-        collect((me + o) % T).wait_send()
+    for o in range(T):
+        for core in (p, 1 - p)[0 if o else 1:]:
+            collect(o, core).wait_send()
 
 
 def shards(observed, baseline, cotangent, first_weight, first_bias, second_weight, second_bias):
@@ -402,9 +403,9 @@
             pltpu.VMEM((2, 8, 16, C), BF16), pltpu.VMEM((2, 2, 16, C), BF16),
             pltpu.VMEM((3, 384, C), F32), pltpu.VMEM((3, 96, C), F32),
             tiles(22, F32), tiles(22, F32),
-            pltpu.VMEM((16, 2, 8, C), F32), pltpu.VMEM((16, 8, C), F32), pltpu.VMEM((16, 8, C), F32),
-            dma((8,)), dma((2,)), dma((2,)), dma((2, T)), dma((2, T)), dma((8, 2)), dma((8, 2)), dma((2,)), dma((2,)),
-            dma((2,)), dma((2,)), dma((T,)), dma((T,)),
+            pltpu.VMEM((16, 2, 8, C), BF16), pltpu.VMEM((2, 16, 8, C), BF16),
+            dma((8,)), dma((2,)), dma((2,)), dma((2, T)), dma((2, T)), dma((10, 2)), dma((10, 2)), dma((2,)), dma((2,)),
+            dma((T, 2)), dma((T, 2)), *[pltpu.SemaphoreType.REGULAR] * 6,
         ],
         compiler_params=pltpu.CompilerParams(collective_id=0, has_side_effects=True),
     )(observed, baseline, cotangent, first_weight, first_bias.reshape(1, C), second_weight,

time: 66.1 us -> 63.4 us (0.959)
  Pallas kernels: 61.8 us -> 59.1 us
    pallas_call x1, Pallas kernels: 61.8 us -> 59.1 us  [shards(): pl.pallas_call(kernel, out_shape=jax.ShapeDtypeStruct((8, 16, C), BF16),...]
where the time goes in v4:
time: 63.4 us; the launch traced here: 63.2 us
  Pallas kernels  59.1 us (93%)
  local copies, waits for them, and re-layouts  4.06 us (6%)
    pallas_call x1, Pallas kernels, shards(): pl.pallas_call(kernel, out_shape=jax.ShapeDtypeStruct((8, 16, C), BF16),...  59.1 us
    unnamed x1, local copies, waits for them, and re-layouts  1.54 us
    reshape x1, local copies, waits for them, and re-layouts, shards(): second_bias.reshape(1, C)  1.28 us

profile of v4, /device:TPU:1, one launch (start us, length us, event | category | flops | bytes accessed | tf_op | source)
XLA Modules:
  0.0 63.2 jit_solution(5363560690359369304)
XLA Ops:
  0.0 1.2 %reshape.6.b1_h = f32[1,384]{1,0:T(1,128)} reshape(f32[384]{0:T(512)} %param.12) | data formatting | bytes 3072 | tf_op jit(solution)/shard_map/reshape | solution.py:411
  1.2 1.3 %reshape.7.b2_h = f32[1,384]{1,0:T(1,128)} reshape(f32[384]{0:T(512)} %param.14) | data formatting | bytes 3072 | tf_op jit(solution)/shard_map/reshape | solution.py:412
  2.5 59.1 %shard_map.82 = bf16[8,16,384]{2,1,0:T(8,128)(2,1)} custom-call(bf16[16,16,384]{2,1,0:T(8,128)(2,1)} %obs_h.1, bf16[16,16,384]{2,1,0:T(8,128)(2,1)} %base_h.1, bf16[16,16,384]{2,1,0:T(8,128)(2,1)} %cot_h.1, bf16[9,192,384]{2,1,0:T(8,128)(2,1)} %w1_h.1, f32[1,384]{1,0:T(1,128)} %reshape.6.b1_h, bf16[9,192,384]{2,1,0:T(8,128)(2,1)} %w2_h.1, ...), custom_call_target="tpu_custom_call" | custom-call | tf_op jit(solution)/shard_map/pallas_call | solution.py:393
  61.7 1.5 %copy.10 = bf16[8,16,384]{2,1,0:T(8,128)(2,1)} copy(bf16[8,16,384]{2,1,0:T(8,128)(2,1)} %shard_map.82) | data formatting | bytes 196608

commit v5 on v4

--- a/solution.py
+++ b/solution.py
@@ -160,9 +160,6 @@
     push_w = [remote(src, dst.at[:, half, :], ws.at[i], wr.at[i], {"path": 1 - p})
               for i, (src, dst) in enumerate(((w1_h, w1), (w2_h, w2)))]
     push_w[0].start()
-    for o in range(1, T):
-        spread(1, o).start()
-    push_w[1].start()
     x[3 + me] = snd[0, me]
     ct[3 + me] = snd[1, me]
 
@@ -251,10 +248,10 @@
                 total = total + (dot if forward else dot_t)(window, weights[3 * (i + 1) + j + 1])
         return total
 
-    def far_conv(parts, start, count, weights, forward):
+    def far_conv(parts, start, count, weights, forward, columns):
         total = jnp.zeros((16 * count, C), F32)
         sign = 1 if forward else -1
-        for j in (0, -1, 1):
+        for j in columns:
             for i in (-1, 0, 1):
                 window = parts[1 + sign * j][pl.ds(start + sign * i, count)].reshape(16 * count, C)
                 total = total + (dot if forward else dot_t)(window, weights[3 * (i + 1) + j + 1])
@@ -265,6 +262,9 @@
 
     seam(0).start()
     give_edges(0, x, nl, nr, 0)
+    for o in range(1, T):
+        spread(1, o).start()
+    push_w[1].start()
     centre(x)
     own_w[0].wait()
     push_w[0].wait_recv()
@@ -285,49 +285,51 @@
     seam(0, True).wait_recv()
     give_far_edges(1, x, nl, nr, 0)
 
-    def second_forward(start, count):
+    def second_forward(start, count, stage):
         window = pl.ds(start, count)
-        _, der = gelu_parts(far_conv((hl, h, hr), start, count, w2, True) + b2_ref[...])
+        total = far_conv((hl, h, hr), start, count, w2, True, (0,))
+        take(stage)
+        _, der = gelu_parts(total + far_conv((hl, h, hr), start, count, w2, True, (-1, 1)) + b2_ref[...])
         a[window] = (der * ct[window].reshape(16 * count, C).astype(F32)).astype(BF16).reshape(count, 16, C)
 
-    take(2)
     early = 3 + 9 * zhi
-    second_forward(early, 7)
+    second_forward(early, 7, 2)
     give_block(4, a, al, ar, early, 7)
-    take(8)
-    early = 10 - 5 * zhi
-    second_forward(early, 7)
-    give_block(9, a, al, ar, early, 7)
-
+    centre_far(x)
+    late = 18 * (1 - zhi)
+    rows = pl.ds(pl.multiple_of(16 * late, 16), 96)
+    qf[1] = qs[1, rows]
+    total = near_conv(qf, 16, 64, w1, True, (0,))
     take(1)
-    centre_far(x)
     sides_far(x, nl, nr)
-    late = 18 * (1 - zhi)
-    for j in range(3):
-        qf[j] = qs[j, pl.ds(pl.multiple_of(16 * late, 16), 96)]
-    act, der = gelu_parts(near_conv(qf, 16, 64, w1, True, (-1, 0, 1)) + b1_ref[...])
+    for j in (0, 2):
+        qf[j] = qs[j, rows]
+    act, der = gelu_parts(total + near_conv(qf, 16, 64, w1, True, (-1, 1)) + b1_ref[...])
     window = pl.ds(late, 4)
     slope[window] = der.reshape(4, 16, C)
     h[window] = (x[window].reshape(64, C).astype(F32) + act).astype(BF16).reshape(4, 16, C)
     give_block(3, h, hl, hr, late, 4)
+
+    early = 10 - 5 * zhi
+    second_forward(early, 7, 8)
+    give_block(9, a, al, ar, early, 7)
+
     seam(1, True).wait_recv()
-    take(3)
     late = 17 - 16 * zhi
-    second_forward(late, 4)
+    second_forward(late, 4, 3)
     give_block(5, a, al, ar, late, 4)
 
-    def second_adjoint(start, count):
+    def second_adjoint(start, count, stage):
         window = pl.ds(start, count)
-        hidden_adj = ct[window].reshape(16 * count, C).astype(F32) + far_conv((al, a, ar), start, count, w2, False)
+        total = ct[window].reshape(16 * count, C).astype(F32) + far_conv((al, a, ar), start, count, w2, False, (0,))
+        take(stage)
+        hidden_adj = total + far_conv((al, a, ar), start, count, w2, False, (-1, 1))
         adj[window] = hidden_adj.reshape(count, 16, C)
         f[window] = (slope[window].reshape(16 * count, C) * hidden_adj).astype(BF16).reshape(count, 16, C)
 
-    take(4)
-    second_adjoint(3 + 10 * zhi, 6)
-    take(9)
-    second_adjoint(9 - 3 * zhi, 7)
-    take(5)
-    second_adjoint(16 - 14 * zhi, 4)
+    second_adjoint(3 + 10 * zhi, 6, 4)
+    second_adjoint(9 - 3 * zhi, 7, 9)
+    second_adjoint(16 - 14 * zhi, 4, 5)
 
     give_edges(6, f, ml, mr, 1)
     give_far_edges(7, f, ml, mr, 1)

time: 63.4 us -> 61 us (0.962)
  Pallas kernels: 59.1 us -> 56.8 us
    pallas_call x1, Pallas kernels: 59.1 us -> 56.8 us  [shards(): pl.pallas_call(kernel, out_shape=jax.ShapeDtypeStruct((8, 16, C), BF16),...]
where the time goes in v5:
time: 61 us; the launch traced here: 60.9 us
  Pallas kernels  56.8 us (93%)
  local copies, waits for them, and re-layouts  4.06 us (7%)
    pallas_call x1, Pallas kernels, shards(): pl.pallas_call(kernel, out_shape=jax.ShapeDtypeStruct((8, 16, C), BF16),...  56.8 us
    unnamed x1, local copies, waits for them, and re-layouts  1.54 us
    reshape x1, local copies, waits for them, and re-layouts, shards(): second_bias.reshape(1, C)  1.28 us
    reshape x1, local copies, waits for them, and re-layouts, shards(): first_bias.reshape(1, C)  1.24 us

profile of v5, /device:TPU:1, one launch (start us, length us, event | category | flops | bytes accessed | tf_op | source)
XLA Modules:
  0.0 60.9 jit_solution(855576329965049124)
XLA Ops:
  0.0 1.2 %reshape.6.b1_h = f32[1,384]{1,0:T(1,128)} reshape(f32[384]{0:T(512)} %param.12) | data formatting | bytes 3072 | tf_op jit(solution)/shard_map/reshape | solution.py:413
  1.2 1.3 %reshape.7.b2_h = f32[1,384]{1,0:T(1,128)} reshape(f32[384]{0:T(512)} %param.14) | data formatting | bytes 3072 | tf_op jit(solution)/shard_map/reshape | solution.py:414
  2.5 56.8 %shard_map.82 = bf16[8,16,384]{2,1,0:T(8,128)(2,1)} custom-call(bf16[16,16,384]{2,1,0:T(8,128)(2,1)} %obs_h.1, bf16[16,16,384]{2,1,0:T(8,128)(2,1)} %base_h.1, bf16[16,16,384]{2,1,0:T(8,128)(2,1)} %cot_h.1, bf16[9,192,384]{2,1,0:T(8,128)(2,1)} %w1_h.1, f32[1,384]{1,0:T(1,128)} %reshape.6.b1_h, bf16[9,192,384]{2,1,0:T(8,128)(2,1)} %w2_h.1, ...), custom_call_target="tpu_custom_call" | custom-call | tf_op jit(solution)/shard_map/pallas_call | solution.py:395
  59.3 1.5 %copy.10 = bf16[8,16,384]{2,1,0:T(8,128)(2,1)} copy(bf16[8,16,384]{2,1,0:T(8,128)(2,1)} %shard_map.82) | data formatting | bytes 196608

commit v6 on v5

--- a/solution.py
+++ b/solution.py
@@ -294,7 +294,7 @@
 
     early = 3 + 9 * zhi
     second_forward(early, 7, 2)
-    give_block(4, a, al, ar, early, 7)
+    first = early
     centre_far(x)
     late = 18 * (1 - zhi)
     rows = pl.ds(pl.multiple_of(16 * late, 16), 96)
@@ -309,6 +309,7 @@
     slope[window] = der.reshape(4, 16, C)
     h[window] = (x[window].reshape(64, C).astype(F32) + act).astype(BF16).reshape(4, 16, C)
     give_block(3, h, hl, hr, late, 4)
+    give_block(4, a, al, ar, first, 7)
 
     early = 10 - 5 * zhi
     second_forward(early, 7, 8)

time: 61 us -> 60 us (0.984)
  Pallas kernels: 56.8 us -> 55.8 us
    pallas_call x1, Pallas kernels: 56.8 us -> 55.8 us  [shards(): pl.pallas_call(kernel, out_shape=jax.ShapeDtypeStruct((8, 16, C), BF16),...]
where the time goes in v6:
time: 60 us; the launch traced here: 59.8 us
  Pallas kernels  55.8 us (93%)
  local copies, waits for them, and re-layouts  4.06 us (7%)
    pallas_call x1, Pallas kernels, shards(): pl.pallas_call(kernel, out_shape=jax.ShapeDtypeStruct((8, 16, C), BF16),...  55.8 us
    unnamed x1, local copies, waits for them, and re-layouts  1.54 us
    reshape x1, local copies, waits for them, and re-layouts, shards(): second_bias.reshape(1, C)  1.28 us
    reshape x1, local copies, waits for them, and re-layouts, shards(): first_bias.reshape(1, C)  1.24 us

profile of v6, /device:TPU:1, one launch (start us, length us, event | category | flops | bytes accessed | tf_op | source)
XLA Modules:
  0.0 59.8 jit_solution(13592254930902239279)
XLA Ops:
  0.0 1.2 %reshape.6.b1_h = f32[1,384]{1,0:T(1,128)} reshape(f32[384]{0:T(512)} %param.12) | data formatting | bytes 3072 | tf_op jit(solution)/shard_map/reshape | solution.py:414
  1.2 1.3 %reshape.7.b2_h = f32[1,384]{1,0:T(1,128)} reshape(f32[384]{0:T(512)} %param.14) | data formatting | bytes 3072 | tf_op jit(solution)/shard_map/reshape | solution.py:415
  2.5 55.8 %shard_map.82 = bf16[8,16,384]{2,1,0:T(8,128)(2,1)} custom-call(bf16[16,16,384]{2,1,0:T(8,128)(2,1)} %obs_h.1, bf16[16,16,384]{2,1,0:T(8,128)(2,1)} %base_h.1, bf16[16,16,384]{2,1,0:T(8,128)(2,1)} %cot_h.1, bf16[9,192,384]{2,1,0:T(8,128)(2,1)} %w1_h.1, f32[1,384]{1,0:T(1,128)} %reshape.6.b1_h, bf16[9,192,384]{2,1,0:T(8,128)(2,1)} %w2_h.1, ...), custom_call_target="tpu_custom_call" | custom-call | tf_op jit(solution)/shard_map/pallas_call | solution.py:396
  58.3 1.5 %copy.10 = bf16[8,16,384]{2,1,0:T(8,128)(2,1)} copy(bf16[8,16,384]{2,1,0:T(8,128)(2,1)} %shard_map.82) | data formatting | bytes 196608
